TPU v7x, 32 devices: a whole 2x2x4 slice. The times are simulated.
32 devices in a mesh: dp: 8 (over z, x), tensor: 4 (over y, core).
Axes of the slice: x: 2, y: 2, z: 4, core: 2. Of those that a mesh axis runs over, the one named last changes fastest.
Arguments:
- x_in: bfloat16 [4096, 1024], P('dp', 'tensor'), may hold values from -6 to 6
- cotangent: bfloat16 [4096, 1024], P('dp', 'tensor'), may hold values from -6 to 6
- seq_ids: int32 [4096], P('dp'), may hold values from -1 to 4095, as said below
- norm_gain: bfloat16 [1024], P('dp'), may hold values from 0.5 to 1.5
- w_zx: bfloat16 [1024, 2, 2048], P('dp', None, 'tensor'), may hold values from -0.1875 to 0.1875
- w_bc: bfloat16 [1024, 256], P('dp', 'tensor'), may hold values from -0.1875 to 0.1875
- w_dt: bfloat16 [1024, 32], P('dp', 'tensor'), may hold values from -0.1875 to 0.1875
- w_out_t: bfloat16 [1024, 2048], P('dp', 'tensor'), may hold values from -0.125 to 0.125
- conv_x_weight: float32 [4, 2048], P(None, 'tensor'), may hold values from -3 to 3
- conv_x_bias: float32 [2048], P('tensor'), may hold values from -3 to 3
- conv_bc_weight: float32 [4, 256], P(None, 'tensor'), may hold values from -3 to 3
- conv_bc_bias: float32 [256], P('tensor'), may hold values from -3 to 3
- dt_bias: float32 [32], P('tensor'), may hold values from -6.9 to -2.25
- a_log: float32 [32], P('tensor'), may hold values from 0 to 2.77
- d_skip: float32 [32], P('tensor'), may hold values from 0.5 to 1.5
- gate_gain: float32 [2048], P('tensor'), may hold values from 0.5 to 1.5
Outputs:
- output: bfloat16 [4096, 1024], P('dp', 'tensor')
- input_grad: float32 [4096, 1024], P('dp', 'tensor')
- grad_norm_gain: float32 [1024], P('dp')
- grad_w_zx: float32 [1024, 2, 2048], P('dp', None, 'tensor')
- grad_w_bc: float32 [1024, 256], P('dp', 'tensor')
- grad_w_dt: float32 [1024, 32], P('dp', 'tensor')
- grad_w_out_t: float32 [1024, 2048], P('dp', 'tensor')
- grad_conv_x_weight: float32 [4, 2048], P(None, 'tensor')
- grad_conv_x_bias: float32 [2048], P('tensor')
- grad_conv_bc_weight: float32 [4, 256], P(None, 'tensor')
- grad_conv_bc_bias: float32 [256], P('tensor')
- grad_dt_bias: float32 [32], P('tensor')
- grad_a_log: float32 [32], P('tensor')
- grad_d_skip: float32 [32], P('tensor')
- grad_gate_gain: float32 [2048], P('tensor')
Inputs may be any that keep to these rules, and one draw needn't show every extreme that they name: `seq_ids`: each entry is -1 for an empty slot or the row index at which its sequence begins. In each block of 512 rows (the rows of one dp index) the live rows come first, their ids never fall, the empty slots follow, and every sequence lies inside one block; the last block has no empty slot and its last row begins a sequence of one row; some other blocks have empty slots.
All inputs are finite; a program needn't handle non-finite values.
Results may differ from a plain program's by a relative error of at most 0.017.
Values may be sent and summed in bfloat16 or wider, within the bound.
A program may use at most 128 MiB of HBM per device.

v0:
```python
from functools import partial

import jax
import jax.numpy as jnp
from jax import lax
from jax.experimental import pallas as pl
from jax.experimental.pallas import tpu as pltpu
from jax.sharding import PartitionSpec as P

HEAD_DIM = 64
PAIR = 2 * HEAD_DIM
EPSILON = 1e-05
PRECISE = lax.Precision.HIGHEST
F32 = jnp.float32
BF16 = jnp.bfloat16


def rows_product(left, right):
    return lax.dot_general(left, right, (((0,), (0,)), ((), ())), preferred_element_type=F32)


def cols_product(left, right):
    return lax.dot_general(left, right, (((1,), (1,)), ((), ())), preferred_element_type=F32)


def plain_product(left, right):
    return lax.dot_general(left, right, (((1,), (0,)), ((), ())), preferred_element_type=F32)


def conv_raw(source, taps, bias, masks):
    count = taps.shape[0]
    summed = bias + taps[count - 1 : count, :] * source
    for shift in range(1, count):
        summed = summed + taps[count - 1 - shift : count - shift, :] * (
            pltpu.roll(source, shift, 0) * masks[:, shift : shift + 1]
        )
    return summed


def conv_back(d_act, source, value, taps, masks):
    count = taps.shape[0]
    rows = source.shape[0]
    logistic = jax.nn.sigmoid(value)
    d_value = d_act * (logistic * (1.0 + value * (1.0 - logistic)))
    d_source = taps[count - 1 : count, :] * d_value
    tap_rows = [jnp.sum(d_value * source, axis=0, keepdims=True)]
    for shift in range(1, count):
        held = d_value * masks[:, shift : shift + 1]
        tap_rows.append(jnp.sum(held * pltpu.roll(source, shift, 0), axis=0, keepdims=True))
        d_source = d_source + taps[count - 1 - shift : count - shift, :] * pltpu.roll(
            held, rows - shift, 0
        )
    d_taps = jnp.concatenate(tap_rows[::-1], axis=0)
    return d_source, d_taps, jnp.sum(d_value, axis=0, keepdims=True)


def two_wide(columns, first):
    return jnp.where(first, columns[:, 0:1], columns[:, 1:2])


def forward_kernel(
    z_ref, x_ref, b_ref, c_ref, taps_ref, bias_ref, mask_ref, seg_ref, segt_ref,
    step_ref, cum_ref, cumt_ref, skip_ref, gain_ref, dq_ref,
    act_ref, y_ref, q_ref, stat_ref, scores,
):
    pair = pl.program_id(0)
    rows = z_ref.shape[0]
    half = rows // 2

    @pl.when(pair == 0)
    def _():
        full = cols_product(c_ref[...], b_ref[...])
        at_row = lax.broadcasted_iota(jnp.int32, full.shape, 0)
        at_col = lax.broadcasted_iota(jnp.int32, full.shape, 1)
        linked = (at_row >= at_col) & (seg_ref[...] == segt_ref[...])
        scores[...] = jnp.where(linked, full, 0.0)
        stat_ref[...] = jnp.zeros_like(stat_ref)

    value = conv_raw(x_ref[...].astype(F32), taps_ref[...], bias_ref[...], mask_ref[...])
    act = (value * jax.nn.sigmoid(value)).astype(BF16)
    act_ref[...] = act
    act_float = act.astype(F32)
    first = lax.broadcasted_iota(jnp.int32, act.shape, 1) < HEAD_DIM
    stepped = act_float * two_wide(step_ref[0], first)
    parts = (
        jnp.where(first, stepped, 0.0).astype(BF16),
        jnp.where(first, 0.0, stepped).astype(BF16),
    )
    for low, wide in ((0, half), (half, rows)):
        total = skip_ref[...] * act_float[low : low + half]
        for head in range(2):
            spread = (
                cum_ref[0, low : low + half, head : head + 1] - cumt_ref[0, head : head + 1, :wide]
            )
            weights = scores[low : low + half, :wide] * jnp.exp(jnp.minimum(spread, 0.0))
            total = total + plain_product(weights.astype(BF16), parts[head][:wide])
        y_ref[low : low + half, :] = total
    z_float = z_ref[...].astype(F32)
    gated = y_ref[...] * (z_float * jax.nn.sigmoid(z_float))
    q = (gated * gain_ref[...]).astype(BF16)
    q_ref[...] = q
    squares = jnp.sum(gated * gated, axis=1, keepdims=True)
    inner = jnp.sum(q.astype(F32) * dq_ref[...], axis=1, keepdims=True)
    pick = lax.broadcasted_iota(jnp.int32, stat_ref.shape, 1) == 0
    stat_ref[...] += jnp.where(pick, squares, inner)


def backward_kernel(
    z_ref, x_ref, b_ref, c_ref, taps_ref, bias_ref, mask_ref, seg_ref, segt_ref,
    step_ref, cum_ref, cumt_ref, skip_ref, gain_ref, dq_ref, act_ref, y_ref, scale_ref,
    dz_ref, dx_ref, dbc_ref, dtaps_ref, sums_ref, dstep_ref, rowsum_ref, colsum_ref,
    scores, d_scores,
):
    pair = pl.program_id(0)
    rows = z_ref.shape[0]
    half = rows // 2

    @pl.when(pair == 0)
    def _():
        full = cols_product(b_ref[...], c_ref[...])
        at_row = lax.broadcasted_iota(jnp.int32, full.shape, 0)
        at_col = lax.broadcasted_iota(jnp.int32, full.shape, 1)
        linked = (at_row <= at_col) & (seg_ref[...] == segt_ref[...])
        scores[...] = jnp.where(linked, full, 0.0)
        d_scores[...] = jnp.zeros_like(d_scores)

    z_float = z_ref[...].astype(F32)
    y = y_ref[...]
    logistic = jax.nn.sigmoid(z_float)
    z_silu = z_float * logistic
    gated = y * z_silu
    d_q = dq_ref[...] * scale_ref[:, 0:1]
    d_gated = d_q * gain_ref[...] - gated * scale_ref[:, 1:2]
    d_y = d_gated * z_silu
    dz_ref[...] = (d_gated * y * (logistic * (1.0 + z_float * (1.0 - logistic)))).astype(BF16)

    act = act_ref[...].astype(F32)
    first = lax.broadcasted_iota(jnp.int32, act.shape, 1) < HEAD_DIM
    step_wide = two_wide(step_ref[0], first)
    stepped = (act * step_wide).astype(BF16)
    parts = (
        jnp.where(first, d_y, 0.0).astype(BF16),
        jnp.where(first, 0.0, d_y).astype(BF16),
    )
    for low, start in ((0, 0), (half, half)):
        held = slice(low, low + half)
        total = jnp.zeros((half, PAIR), F32)
        for head in range(2):
            spread = cumt_ref[0, head : head + 1, start:] - cum_ref[0, held, head : head + 1]
            decay = jnp.exp(jnp.minimum(spread, 0.0))
            weights = scores[held, start:] * decay
            total = total + plain_product(weights.astype(BF16), parts[head][start:])
            d_weights = cols_product(stepped[held], parts[head][start:])
            d_scores[held, start:] += d_weights * decay
            d_spread = d_weights * weights
            colsum_ref[0, held, head : head + 1] = jnp.sum(d_spread, axis=1, keepdims=True)
            along = jnp.sum(d_spread, axis=0, keepdims=True)
            if low == 0:
                rowsum_ref[0, head : head + 1, :] = along
            else:
                rowsum_ref[0, head : head + 1, start:] += along
        direct = total * act[held]
        dstep_ref[0, held, 0:1] = jnp.sum(
            jnp.where(first[held], direct, 0.0), axis=1, keepdims=True
        )
        dstep_ref[0, held, 1:2] = jnp.sum(
            jnp.where(first[held], 0.0, direct), axis=1, keepdims=True
        )
        y_ref[held, :] = total * step_wide[held]
    d_act = y_ref[...] + skip_ref[...] * d_y
    source = x_ref[...].astype(F32)
    value = conv_raw(source, taps_ref[...], bias_ref[...], mask_ref[...])
    d_source, d_taps, d_bias = conv_back(d_act, source, value, taps_ref[...], mask_ref[...])
    dx_ref[...] = d_source.astype(BF16)
    dtaps_ref[...] = d_taps
    sums_ref[0:1, :] = d_bias
    sums_ref[1:2, :] = jnp.sum(d_q * gated, axis=0, keepdims=True)
    sums_ref[2:3, :] = jnp.sum(d_y * act, axis=0, keepdims=True)

    @pl.when(pair == pl.num_programs(0) - 1)
    def _():
        at_row = lax.broadcasted_iota(jnp.int32, d_scores.shape, 0)
        at_col = lax.broadcasted_iota(jnp.int32, d_scores.shape, 1)
        linked = (at_row <= at_col) & (seg_ref[...] == segt_ref[...])
        held = jnp.where(linked, d_scores[...], 0.0).astype(BF16)
        width = b_ref.shape[1]
        dbc_ref[:, :width] = plain_product(held, c_ref[...]).astype(BF16)
        dbc_ref[:, width:] = rows_product(held, b_ref[...]).astype(BF16)


def meet(barrier):
    count = lax.axis_size("tensor")
    for away in range(1, count):
        to = lax.rem(lax.axis_index("tensor") + away, count)
        pl.semaphore_signal(barrier, inc=1, device_id={"tensor": to}, device_id_type=MESH)
    pl.semaphore_wait(barrier, count - 1)


def tensor_sum_kernel(in_ref, out_ref, slots, sems):
    meet(pltpu.get_barrier_semaphore())
    copies = all_to(in_ref, slots, "tensor", sems, 0)
    for copy in copies:
        copy.start()
    total = in_ref[...]
    for away, copy in enumerate(copies):
        copy.wait()
        total = total + slots[away]
    out_ref[...] = total


def bc_conv_kernel(pre_ref, taps_ref, bias_ref, mask_ref, act_ref):
    value = conv_raw(pre_ref[...].astype(F32), taps_ref[...], bias_ref[...], mask_ref[...])
    act_ref[...] = (value * jax.nn.sigmoid(value)).astype(BF16)


def bc_back_kernel(
    d_ref, pre_ref, taps_ref, bias_ref, mask_ref, dpre_ref, dtaps_ref, dbias_ref, slots, sems
):
    count = lax.axis_size("tensor")
    me = lax.axis_index("tensor")
    cols = pre_ref.shape[1]
    slab = slots.shape[2]
    fold = slab // cols

    def place(index):
        return pl.ds(pl.multiple_of(index // fold * slab, slab), slab)

    def part(away):
        to = lax.rem(me + away, count)
        return remote(
            d_ref.at[:, place(to)], slots.at[away - 1], sems.at[0, away], sems.at[1, away],
            "tensor", to,
        )

    meet(pltpu.get_barrier_semaphore())
    for away in range(1, count):
        part(away).start()
    wide = d_ref[:, place(me)].astype(F32)
    for away in range(1, count):
        part(away).wait()
        wide = wide + slots[away - 1].astype(F32)
    d_own = wide[:, :cols]
    for piece in range(1, fold):
        d_own = jnp.where(
            me % fold == piece, wide[:, piece * cols : (piece + 1) * cols], d_own
        )
    source = pre_ref[...].astype(F32)
    value = conv_raw(source, taps_ref[...], bias_ref[...], mask_ref[...])
    d_source, d_taps, d_bias = conv_back(d_own, source, value, taps_ref[...], mask_ref[...])
    dpre_ref[...] = d_source.astype(BF16)
    dtaps_ref[...] = d_taps
    dbias_ref[...] = d_bias


MESH = pl.DeviceIdType.MESH


def lines(axis):
    count = lax.axis_size(axis)
    low = 2 if count % 2 == 0 else 1
    me = lax.axis_index(axis)
    return me, me // low, me % low, count // low, low


def remote(source, target, send, recv, axis, index):
    return pltpu.make_async_remote_copy(
        src_ref=source,
        dst_ref=target,
        send_sem=send,
        recv_sem=recv,
        device_id={axis: index},
        device_id_type=MESH,
    )


def greet_all(barrier):
    peers = 0
    for axis in ("dp", "tensor"):
        count = lax.axis_size(axis)
        for away in range(1, count):
            to = lax.rem(lax.axis_index(axis) + away, count)
            pl.semaphore_signal(barrier, inc=1, device_id={axis: to}, device_id_type=MESH)
        peers += count - 1
    pl.semaphore_wait(barrier, peers)


class Line:
    def __init__(self, axis, slot, sems):
        self.axis, self.slot, self.sems = axis, slot, sems
        self.me, self.high, self.low, self.highs, self.lows = lines(axis)

    def index(self, high, low):
        return high * self.lows + low

    def has(self, way, steps):
        if way == 0:
            return self.high - steps >= 0
        return self.high + steps < self.highs

    def towards(self, way, steps):
        return self.high - steps if way == 0 else self.high + steps

    def hop(self, way, step, low):
        block = self.slot(self.index(self.towards(way, step - 1), low))
        onto = self.index(self.towards(1 - way, 1), self.low)
        return remote(
            block, block, self.sems.at[0, way, step], self.sems.at[1, way, step], self.axis, onto
        )

    def across(self, way, steps):
        block = self.slot(self.index(self.towards(way, steps), self.low))
        onto = self.index(self.high, 1 - self.low)
        return remote(
            block, block, self.sems.at[2, way, steps], self.sems.at[3, way, steps], self.axis, onto
        )

    def sends(self, way, step):
        return self.has(1 - way, 1) & self.has(way, step - 1)

    def step(self, step):
        for way in range(2):
            if step == 0:
                pl.when(self.sends(way, 1))(lambda way=way: self.hop(way, 1, self.low).start())
                continue

            @pl.when(self.has(way, step))
            def _(way=way):
                self.hop(way, step, self.low).wait_recv()
                if step + 1 < self.highs:
                    pl.when(self.sends(way, step + 1))(
                        lambda: self.hop(way, step + 1, self.low).start()
                    )
                if self.lows == 2:
                    self.across(way, step).start()

        if step == 0 and self.lows == 2:
            self.across(0, 0).start()

    def finish(self):
        for step in range(1, self.highs):
            for way in range(2):
                pl.when(self.sends(way, step))(
                    lambda way=way, step=step: self.hop(way, step, self.low).wait_send()
                )
        if self.lows == 2:
            self.across(0, 0).wait()
            for step in range(1, self.highs):
                for way in range(2):
                    pl.when(self.has(way, step))(
                        lambda way=way, step=step: self.across(way, step).wait()
                    )


def gather_kernel(w_ref, xc_ref, wide_ref, rows_ref, dp_sems, tensor_sems, own_sems):
    deep = w_ref.shape[0]
    share = xc_ref.shape[1]

    def dp_slot(index):
        return wide_ref.at[index]

    def tensor_slot(index):
        return rows_ref.at[:, pl.ds(pl.multiple_of(index * share, share), share)]

    dp = Line("dp", dp_slot, dp_sems)
    tensor = Line("tensor", tensor_slot, tensor_sems)
    barrier = pltpu.get_barrier_semaphore()
    own = (
        pltpu.make_async_copy(w_ref, dp_slot(dp.me), own_sems.at[0]),
        pltpu.make_async_copy(xc_ref, tensor_slot(tensor.me), own_sems.at[1]),
    )
    for copy in own:
        copy.start()
    greet_all(barrier)
    for copy in own:
        copy.wait()
    for step in range(max(dp.highs, tensor.highs)):
        for line in (dp, tensor):
            if step < line.highs:
                line.step(step)
    tensor.finish()
    dp.finish()


def all_to(ref, slots, axis, sems, base):
    count = lax.axis_size(axis)
    me = lax.axis_index(axis)
    return [
        remote(
            ref, slots.at[away - 1], sems.at[0, base + away], sems.at[1, base + away], axis,
            lax.rem(me + away, count),
        )
        for away in range(1, count)
    ]


def sum_kernel(
    grads_ref, norm_ref, out_ref, small_ref, mean_ref,
    zx_ref, bc_ref, dt_ref, weight_ref, norm_share_ref, out_share_ref, small_sum_ref, gain_sum_ref,
    mean_sum_ref, share_ref, paired, held, landed, norm_slots, out_slots, small_slots, gain_slots, mean_slots, gain_ref,
    pair_sems, line_sems, norm_sems, small_sems, tensor_sems,
):
    me, high, low, highs, lows = lines("dp")
    count = lax.axis_size("dp")
    tensor_count = lax.axis_size("tensor")
    tensor_me = lax.axis_index("tensor")
    share = norm_share_ref.shape[1]
    barrier = pltpu.get_barrier_semaphore()
    greet_all(barrier)

    order = sorted(range(highs), key=lambda k: (k == 0, -min(k, highs - k)))
    partner = high * lows + (lows - 1 - low)

    def crossing(away):
        to = lax.rem(high + away, highs)
        return remote(
            grads_ref.at[to * lows + (lows - 1 - low)], paired.at[away],
            pair_sems.at[0, away], pair_sems.at[1, away], "dp", partner,
        )

    def going(away):
        to = lax.rem(high + away, highs)
        return remote(
            held.at[away], landed.at[away],
            line_sems.at[0, away], line_sems.at[1, away], "dp", to * lows + low,
        )

    def part(ref, slots, away, which):
        to = lax.rem(tensor_me + away, tensor_count)
        return remote(
            ref.at[:, pl.ds(pl.multiple_of(to * share, share), share)], slots.at[away - 1],
            norm_sems.at[0, which, away], norm_sems.at[1, which, away], "tensor", to,
        )

    small = all_to(small_ref, small_slots, "dp", small_sems, 0)
    mean = all_to(mean_ref, mean_slots, "tensor", tensor_sems, 0)
    for copy in small + mean:
        copy.start()
    if lows == 2:
        for away in order:
            crossing(away).start()
    turns = sorted(range(1, tensor_count), key=lambda k: k % 2)
    for away in turns:
        part(norm_ref, norm_slots, away, 0).start()
    for away in turns:
        part(out_ref, out_slots, away, 1).start()

    for copy in small:
        copy.wait()
    total = small_ref[...]
    for away in range(1, count):
        total = total + small_slots[away - 1]
    small_sum_ref[...] = total
    gain_rows = gain_ref.shape[0]
    gain_ref[...] = total[:gain_rows]
    gain = all_to(gain_ref, gain_slots, "tensor", tensor_sems, tensor_count)
    for copy in gain:
        copy.start()

    for away in order:
        to = lax.rem(high + away, highs)
        both = grads_ref[to * lows + low].astype(F32)
        if lows == 2:
            crossing(away).wait()
            both = both + paired[away].astype(F32)
        if away == 0:
            share_ref[...] = both
        else:
            held[away] = both.astype(BF16)
            going(away).start()

    for copy in mean + gain:
        copy.wait()
    total = mean_ref[...]
    gained = gain_ref[...]
    for away in range(1, tensor_count):
        total = total + mean_slots[away - 1]
        gained = gained + gain_slots[away - 1]
    mean_sum_ref[...] = total
    gain_sum_ref[...] = gained
    for which, ref, slots, result in (
        (0, norm_ref, norm_slots, norm_share_ref),
        (1, out_ref, out_slots, out_share_ref),
    ):
        total = ref[:, pl.ds(pl.multiple_of(tensor_me * share, share), share)].astype(F32)
        for away in range(1, tensor_count):
            part(ref, slots, away, which).wait()
            total = total + slots[away - 1].astype(F32)
        result[...] = total
    for away in order[:-1]:
        going(away).wait()
        share_ref[...] += landed[away].astype(F32)
    zx_cols, bc_cols, dt_cols = zx_ref.shape[1], bc_ref.shape[1], dt_ref.shape[1]
    zx_ref[...] = share_ref[:, :zx_cols]
    bc_ref[...] = share_ref[:, zx_cols : zx_cols + bc_cols]
    dt_ref[...] = share_ref[:, zx_cols + bc_cols : zx_cols + bc_cols + dt_cols]
    weight_ref[...] = share_ref[:, share_ref.shape[1] - weight_ref.shape[1] :]


def shape(dims, dtype=F32):
    return jax.ShapeDtypeStruct(dims, dtype)


def local(
    x_in,
    cotangent,
    seq_ids,
    norm_gain,
    w_zx,
    w_bc,
    w_dt,
    w_out_t,
    conv_x_weight,
    conv_x_bias,
    conv_bc_weight,
    conv_bc_bias,
    dt_bias,
    a_log,
    d_skip,
    gate_gain,
    *,
    tensor_count,
):
    rows, share = x_in.shape
    width = share * tensor_count
    inner = w_out_t.shape[1]
    pairs = inner // PAIR
    heads = w_dt.shape[1]
    bc_cols = w_bc.shape[1]
    taps = conv_x_weight.shape[0]
    held_rows = w_zx.shape[0]
    spare = -(bc_cols + heads + 1) % 128
    side = bc_cols + heads + 1 + spare

    counts = {name: lax.axis_size(name) for name in ("dp", "tensor")}
    highs = {name: -(-counts[name] // 2) if counts[name] % 2 == 0 else counts[name] for name in counts}
    vmem = pl.BlockSpec(memory_space=pltpu.VMEM)
    local_weights = jnp.concatenate(
        [
            w_zx.reshape(held_rows, -1),
            w_bc,
            w_dt,
            norm_gain[:, None],
            jnp.zeros((held_rows, spare), BF16),
            w_out_t,
        ],
        axis=1,
    )
    packs = local_weights.shape[1]
    gathered, both = pl.pallas_call(
        gather_kernel,
        in_specs=[vmem, vmem],
        out_specs=[vmem, vmem],
        out_shape=[
            shape((counts["dp"], held_rows, packs), BF16),
            shape((2 * rows, width), BF16),
        ],
        scratch_shapes=[
            pltpu.SemaphoreType.DMA((4, 2, highs["dp"])),
            pltpu.SemaphoreType.DMA((4, 2, highs["tensor"])),
            pltpu.SemaphoreType.DMA((2,)),
        ],
        compiler_params=pltpu.CompilerParams(collective_id=0, has_side_effects=True),
        name="opening_gather",
    )(local_weights, jnp.concatenate([x_in, cotangent], axis=0))
    gathered = gathered.reshape(counts["dp"] * held_rows, packs)
    packed = gathered[:, : 2 * inner + side]
    out_weight = gathered[:, 2 * inner + side :]

    x_rows, cot_rows = both[:rows], both[rows:]
    col_start = lax.axis_index("tensor") * share
    live = (seq_ids >= 0).astype(F32)
    masks = [live[:, None]]
    for shift in range(1, taps):
        same = (seq_ids[shift:] == seq_ids[:-shift]).astype(F32)
        masks.append(jnp.concatenate([jnp.zeros((shift,), F32), same])[:, None])
    masks = jnp.concatenate(masks, axis=1)
    seg, segt = seq_ids[:, None], seq_ids[None, :]

    gain = packed[:, 2 * inner + bc_cols + heads].astype(F32)
    x_float = x_rows.astype(F32)
    inv_rms = lax.rsqrt(jnp.mean(x_float * x_float, axis=-1) + EPSILON)
    normed = (x_float * inv_rms[:, None] * gain[None, :]).astype(BF16)
    zx = plain_product(normed, packed[:, : 2 * inner]).astype(BF16)
    bcdt = plain_product(normed, packed[:, 2 * inner :])
    bc_pre = bcdt[:, :bc_cols].astype(BF16)
    dt_in = bcdt[:, bc_cols : bc_cols + heads] + dt_bias[None, :]

    bc_local = pl.pallas_call(
        bc_conv_kernel, out_shape=shape((rows, bc_cols), BF16), name="bc_conv"
    )(bc_pre, conv_bc_weight, conv_bc_bias[None, :], masks)
    bc_act = lax.all_gather(bc_local, "tensor", axis=1, tiled=True)
    state = bc_act.shape[1] // 2
    b_matrix, c_matrix = bc_act[:, :state], bc_act[:, state:]

    step = jax.nn.softplus(dt_in)
    rate = -jnp.exp(a_log)
    log_decay = step * rate[None, :]
    at = jnp.arange(rows)
    lower = (at[:, None] >= at[None, :]).astype(F32)
    cumulative = jnp.dot(lower, log_decay, precision=PRECISE)
    step_pairs = step.reshape(rows, pairs, 2).transpose(1, 0, 2)
    cum_pairs = cumulative.reshape(rows, pairs, 2).transpose(1, 0, 2)
    cumt_pairs = cumulative.T.reshape(pairs, 2, rows)
    skip_wide = jnp.repeat(d_skip, HEAD_DIM)[None, :]
    gate_wide = gate_gain[None, :]
    d_q_raw = plain_product(cot_rows, out_weight)

    def whole(dims):
        return pl.BlockSpec(dims, lambda p: (0,) * len(dims))

    columns = pl.BlockSpec((rows, PAIR), lambda p: (0, p))
    row_wide = pl.BlockSpec((1, PAIR), lambda p: (0, p))
    per_pair = pl.BlockSpec((1, rows, 2), lambda p: (p, 0, 0))
    per_pair_t = pl.BlockSpec((1, 2, rows), lambda p: (p, 0, 0))
    common_specs = [
        columns,
        pl.BlockSpec((rows, PAIR), lambda p: (0, p + pairs)),
        whole((rows, state)),
        whole((rows, state)),
        pl.BlockSpec((taps, PAIR), lambda p: (0, p)),
        row_wide,
        whole((rows, taps)),
        whole((rows, 1)),
        whole((1, rows)),
        per_pair,
        per_pair,
        per_pair_t,
        row_wide,
        row_wide,
        columns,
    ]
    common = (
        zx, zx, b_matrix, c_matrix, conv_x_weight, conv_x_bias[None, :], masks, seg, segt,
        step_pairs, cum_pairs, cumt_pairs, skip_wide, gate_wide, d_q_raw,
    )
    x_act, y_flat, q_rows, stats = pl.pallas_call(
        forward_kernel,
        grid=(pairs,),
        in_specs=common_specs,
        out_specs=[columns, columns, columns, whole((rows, 2))],
        out_shape=[
            shape((rows, inner), BF16),
            shape((rows, inner)),
            shape((rows, inner), BF16),
            shape((rows, 2)),
        ],
        scratch_shapes=[pltpu.VMEM((rows, rows), F32)],
        name="mixer_forward",
    )(*common)

    stat_dims = (2 * rows // 128, 128)
    totals = pl.pallas_call(
        tensor_sum_kernel,
        out_shape=shape(stat_dims),
        in_specs=[vmem],
        out_specs=vmem,
        scratch_shapes=[
            pltpu.VMEM((counts["tensor"] - 1,) + stat_dims, F32),
            pltpu.SemaphoreType.DMA((2, counts["tensor"])),
        ],
        compiler_params=pltpu.CompilerParams(collective_id=2, has_side_effects=True),
        name="stat_sum",
    )(stats.T.reshape(stat_dims)).reshape(2, rows)
    partial_out = cols_product(q_rows, out_weight).astype(BF16)
    inner_all = inner * tensor_count
    inv_gate = lax.rsqrt(totals[0] / inner_all + EPSILON)
    row_scale = inv_gate * live
    pull = inv_gate * inv_gate * (totals[1] * row_scale) / inner_all
    scales = jnp.stack([row_scale, pull], axis=1)
    d_scaled = (cot_rows.astype(F32) * row_scale[:, None]).astype(BF16)
    out_grad = rows_product(d_scaled, q_rows).astype(BF16)

    d_z, d_x, d_bc, d_taps, sums, d_step, rowsum, colsum = pl.pallas_call(
        backward_kernel,
        grid=(pairs,),
        in_specs=common_specs + [columns, columns, whole((rows, 2))],
        out_specs=[
            columns,
            columns,
            whole((rows, 2 * state)),
            pl.BlockSpec((taps, PAIR), lambda p: (0, p)),
            pl.BlockSpec((3, PAIR), lambda p: (0, p)),
            per_pair,
            per_pair_t,
            per_pair,
        ],
        out_shape=[
            shape((rows, inner), BF16),
            shape((rows, inner), BF16),
            shape((rows, 2 * state), BF16),
            shape((taps, inner)),
            shape((3, inner)),
            shape((pairs, rows, 2)),
            shape((pairs, 2, rows)),
            shape((pairs, rows, 2)),
        ],
        scratch_shapes=[pltpu.VMEM((rows, rows), F32), pltpu.VMEM((rows, rows), F32)],
        name="mixer_backward",
    )(*common, x_act, y_flat, scales)

    slab = max(bc_cols, 128)
    d_cum = rowsum.reshape(heads, rows).T - colsum.transpose(1, 0, 2).reshape(rows, heads)
    d_decay = lax.dot_general(lower, d_cum, (((0,), (0,)), ((), ())), precision=PRECISE)
    d_step_all = d_step.transpose(1, 0, 2).reshape(rows, heads) + d_decay * rate[None, :]
    d_dt = d_step_all * jax.nn.sigmoid(dt_in)
    d_bcpre, bc_taps_grad, bc_bias_grad = pl.pallas_call(
        bc_back_kernel,
        out_shape=[
            shape((rows, bc_cols), BF16),
            shape((taps, bc_cols)),
            shape((1, bc_cols)),
        ],
        in_specs=[vmem] * 5,
        out_specs=[vmem] * 3,
        scratch_shapes=[
            pltpu.VMEM((counts["tensor"] - 1, rows, slab), BF16),
            pltpu.SemaphoreType.DMA((2, counts["tensor"])),
        ],
        compiler_params=pltpu.CompilerParams(collective_id=3, has_side_effects=True),
        name="bc_conv_back",
    )(d_bc, bc_pre, conv_bc_weight, conv_bc_bias[None, :], masks)

    d_side = jnp.concatenate(
        [d_z, d_x, d_bcpre, d_dt.astype(BF16), jnp.zeros((rows, side - bc_cols - heads), BF16)],
        axis=1,
    )
    pack_grad = rows_product(normed, d_side).astype(BF16)
    d_norm_part = cols_product(d_side, packed)
    x_hat = x_float * inv_rms[:, None]
    weighed = d_norm_part * x_hat
    gain_part = jnp.sum(weighed, axis=0)
    mean_part = jnp.sum(weighed * gain[None, :], axis=1)
    pieces = (
        gain_part,
        d_taps.reshape(-1),
        sums[0],
        bc_taps_grad.reshape(-1),
        bc_bias_grad[0],
        jnp.sum(d_dt, axis=0),
        jnp.sum(d_decay * log_decay, axis=0),
        jnp.sum(sums[2].reshape(heads, HEAD_DIM), axis=1),
        sums[1],
    )
    length = sum(piece.shape[0] for piece in pieces)
    lane = 128
    depth = 8 * -(-length // (8 * lane))
    flat = jnp.concatenate(pieces + (jnp.zeros((depth * lane - length,), F32),))
    gain_rows = width // lane
    mean_rows = -(-rows // lane)
    grads = jnp.concatenate([pack_grad, out_grad], axis=1).reshape(counts["dp"], held_rows, packs)
    dp_high, dp_others, tensor_others = highs["dp"], counts["dp"] - 1, counts["tensor"] - 1
    zx_share, bc_share, dt_share, out_grad_share, d_norm_own, out_share, flat, gain_sum, mean_sum = pl.pallas_call(
        sum_kernel,
        in_specs=[vmem] * 5,
        out_specs=[vmem] * 9,
        out_shape=[
            shape((held_rows, 2 * inner)),
            shape((held_rows, bc_cols)),
            shape((held_rows, heads)),
            shape((held_rows, inner)),
            shape((rows, share)),
            shape((rows, share)),
            shape((depth, lane)),
            shape((gain_rows, lane)),
            shape((mean_rows, lane)),
        ],
        scratch_shapes=[
            pltpu.VMEM((held_rows, packs), F32),
            pltpu.VMEM((dp_high, held_rows, packs), BF16),
            pltpu.VMEM((dp_high, held_rows, packs), BF16),
            pltpu.VMEM((dp_high, held_rows, packs), BF16),
            pltpu.VMEM((tensor_others, rows, share), BF16),
            pltpu.VMEM((tensor_others, rows, share), BF16),
            pltpu.VMEM((dp_others, depth, lane), F32),
            pltpu.VMEM((tensor_others, gain_rows, lane), F32),
            pltpu.VMEM((tensor_others, mean_rows, lane), F32),
            pltpu.VMEM((gain_rows, lane), F32),
            pltpu.SemaphoreType.DMA((2, dp_high)),
            pltpu.SemaphoreType.DMA((2, dp_high)),
            pltpu.SemaphoreType.DMA((2, 2, tensor_others + 1)),
            pltpu.SemaphoreType.DMA((2, dp_others + 1)),
            pltpu.SemaphoreType.DMA((2, 2 * tensor_others + 2)),
        ],
        compiler_params=pltpu.CompilerParams(collective_id=1, has_side_effects=True),
        name="closing_sums",
    )(
        grads,
        d_norm_part.astype(BF16),
        partial_out,
        flat.reshape(depth, lane),
        mean_part.reshape(mean_rows, lane),
    )
    output = (x_in.astype(F32) + out_share * row_scale[:, None]).astype(BF16)
    row_mean = mean_sum.reshape(-1) / width
    gain_own = lax.dynamic_slice_in_dim(gain, col_start, share, 0)
    input_grad = inv_rms[:, None] * (
        d_norm_own * gain_own[None, :]
        - x_in.astype(F32) * (inv_rms * row_mean)[:, None]
    ) + cotangent.astype(F32)
    flat = flat.reshape(-1)
    parts, at_piece = [], 0
    for piece in pieces:
        parts.append(flat[at_piece : at_piece + piece.shape[0]])
        at_piece += piece.shape[0]
    parts = parts[1:]
    gain_share = lax.dynamic_slice_in_dim(
        gain_sum.reshape(-1), lax.axis_index("dp") * held_rows, held_rows, 0
    )
    return (
        output,
        input_grad,
        gain_share,
        zx_share.reshape(held_rows, 2, inner),
        bc_share,
        dt_share,
        out_grad_share,
        parts[0].reshape(taps, inner),
        parts[1],
        parts[2].reshape(taps, bc_cols),
        parts[3],
        parts[4],
        parts[5],
        parts[6],
        parts[7],
    )


def solution(mesh):
    return jax.shard_map(
        partial(local, tensor_count=mesh.shape["tensor"]),
        mesh=mesh,
        in_specs=(
            P("dp", "tensor"),
            P("dp", "tensor"),
            P("dp"),
            P("dp"),
            P("dp", None, "tensor"),
            P("dp", "tensor"),
            P("dp", "tensor"),
            P("dp", "tensor"),
            P(None, "tensor"),
            P("tensor"),
            P(None, "tensor"),
            P("tensor"),
            P("tensor"),
            P("tensor"),
            P("tensor"),
            P("tensor"),
        ),
        out_specs=(
            P("dp", "tensor"),
            P("dp", "tensor"),
            P("dp"),
            P("dp", None, "tensor"),
            P("dp", "tensor"),
            P("dp", "tensor"),
            P("dp", "tensor"),
            P(None, "tensor"),
            P("tensor"),
            P(None, "tensor"),
            P("tensor"),
            P("tensor"),
            P("tensor"),
            P("tensor"),
            P("tensor"),
        ),
        check_vma=False,
    )
```

profile of v0, /device:TPU:0, one launch (start us, length us, event | category | flops | bytes accessed | tf_op | source)
XLA Modules:
  0.0 216.4 jit_solution(1849190274871454034)
XLA Ops:
  0.6 1.0 copy.125
  1.6 0.8 copy.93
  2.5 0.8 copy.94
  3.3 0.8 copy.95
  4.1 1.8 concatenate.30.w_ref
  5.8 1.9 pad_maximum_fusion.1.xc_ref
  7.7 50.5 %opening_gather.1 = (bf16[8,128,1664]{2,1,0:T(8,128)(2,1)}, bf16[1024,1024]{1,0:T(8,128)(2,1)}) custom-call(bf16[128,1664]{1,0:T(8,128)(2,1)} %concatenate.30.w_ref, bf16[1024,256]{1,0:T(8,128)(2,1)} %pad_maximum_fusion.1.xc_ref), custom_call_target="tpu_custom_call" | custom-call | tf_op jit(solution)/shard_map/opening_gather/pallas_call | solution.py:549
  58.3 1.5 fusion.5
  59.8 1.1 slice.132
  61.0 1.8 fusion.26
  62.8 0.7 slice.191.pre_ref
  64.2 0.7 concatenate.36.mask_ref
  64.9 2.0 bc_conv.1
  66.9 1.0 copy.99
  67.9 6.0 %all_gather.3 = bf16[512,256]{0,1:T(8,128)(2,1)S(1)} all-gather(bf16[512,64]{0,1:T(8,128)(2,1)S(1)} %copy.99), channel_id=1, replica_groups=mesh['dp'=8,'tensor'=4] {'tensor'}, dimensions={1}, use_global_device_ids=true | all-gather | bytes 327680 | tf_op jit(solution)/shard_map/all_gather | solution.py:591
  73.9 0.8 copy.123.b_ref
  74.7 0.8 copy.124.c_ref
  76.2 1.5 copy.106
  78.4 1.3 copy.105
  79.8 3.9 %fusion.8.z_ref.x_ref = bf16[512,1024]{1,0:T(8,128)(2,1)} fusion(bf16[1024,1664]{1,0:T(8,128)(2,1)} %bitcast.80, f32[1024]{0:T(1024)S(1)} %bitcast.97, f32[512]{0:T(512)S(1)} %add_rsqrt_fusion.1, bf16[1024,1024]{1,0:T(8,128)(2,1)S(1)} %copy-done.5), kind=kOutput, calls=%fused_computation.14 | convolution fusion | flops 1076363264 | bytes 4200448 | tf_op jit(solution)/shard_map/dot_general | solution.py:27
  83.6 3.0 %fusion.16.dq_ref = f32[512,512]{1,0:T(8,128)} fusion(bf16[1024,1664]{1,0:T(8,128)(2,1)} %bitcast.81, bf16[1024,1024]{1,0:T(8,128)(2,1)S(1)} %copy-done.5), kind=kOutput, calls=%fused_computation.23 | convolution fusion | flops 536870912 | bytes 3145728 | tf_op jit(solution)/shard_map/dot_general | solution.py:27
  86.6 0.9 copy.109.seg_ref
  87.6 0.7 broadcast_in_dim_reshape.3.skip_ref
  88.2 7.5 %mixer_forward.1 = (bf16[512,512]{1,0:T(8,128)(2,1)}, f32[512,512]{1,0:T(8,128)}, bf16[512,512]{1,0:T(8,128)(2,1)}, f32[512,2]{1,0:T(8,128)}) custom-call(bf16[512,1024]{1,0:T(8,128)(2,1)} %fusion.8.z_ref.x_ref, bf16[512,1024]{1,0:T(8,128)(2,1)} %fusion.8.z_ref.x_ref, bf16[512,128]{1,0:T(8,128)(2,1)} %copy.123.b_ref, bf16[512,128]{1,0:T(8,128)(2,1)} %copy.124.c_ref, ...), custom_call_target="tpu_custom_call" | custom-call | tf_op jit(solution)/shard_map/mixer_forward/pallas_call | solution.py:636
  95.8 1.1 copy.108
  97.4 5.0 %stat_sum.1 = f32[8,128]{1,0:T(8,128)} custom-call(f32[8,128]{1,0:T(8,128)} %reshape.134.in_ref), custom_call_target="tpu_custom_call" | custom-call | tf_op jit(solution)/shard_map/stat_sum/pallas_call | solution.py:652
  102.4 0.8 fusion.31
  103.2 0.9 copy.110.scale_ref
  104.1 13.3 %mixer_backward.1 = (bf16[512,512]{1,0:T(8,128)(2,1)}, bf16[512,512]{1,0:T(8,128)(2,1)}, bf16[512,256]{1,0:T(8,128)(2,1)}, f32[4,512]{1,0:T(4,128)}, f32[3,512]{...) custom-call(bf16[512,1024]{1,0:T(8,128)(2,1)} %fusion.8.z_ref.x_ref, ...), custom_call_target="tpu_custom_call" | custom-call | tf_op jit(solution)/shard_map/mixer_backward/pallas_call | solution.py:673
  117.4 1.6 copy.111
  120.3 9.4 %bc_conv_back.1 = (bf16[512,64]{1,0:T(8,128)(2,1)}, f32[4,64]{1,0:T(4,128)}, f32[1,64]{1,0:T(1,128)}) custom-call(bf16[512,256]{1,0:T(8,128)(2,1)} %get-tuple-element.48.d_ref, bf16[512,64]{1,0:T(8,128)(2,1)} %slice.191.pre_ref, f32[4,64]{1,0:T(4,128)} %taps_ref.7, f32[1,64]{1,0:T(1,128)} %bitcast.103, f32[512,4]{1,0:T(8,128)} %concatenate.36.mask_ref), custom_call_target="tpu_custom_call" | custom-call | tf_op jit(solution)/shard_map/bc_conv_back/pallas_call | solution.py:706
  129.8 2.6 %concatenate.37 = bf16[512,1152]{1,0:T(8,128)(2,1)S(1)} concatenate(bf16[512,512]{1,0:T(8,128)(2,1)S(1)} %copy-done.3, bf16[512,512]{1,0:T(8,128)(2,1)S(1)} %copy-done.4, bf16[512,64]{1,0:T(8,128)(2,1)} %get-tuple-element.49, bf16[512,8]{1,0:T(8,128)(2,1)S(1)} %get-tuple-element.130, bf16[512,56]{1,0:T(8,128)(2,1)S(1)} %broadcast_in_dim.73), dimensions={1} | concatenate | bytes 2359296 | tf_op jit(solution)/shard_map/concatenate | solution.py:723
  132.4 5.3 %multiply_reduce_fusion = (f32[512]{0:T(512)}, f32[1024]{0:T(1024)S(1)}, bf16[512,1024]{1,0:T(8,128)(2,1)}) fusion(f32[1024]{0:T(1024)S(1)} %bitcast.98, f32[512]{0:T(512)S(1)} %add_rsqrt_fusion.1, bf16[1024,1024]{1,0:T(8,128)(2,1)} %get-tuple-element.41, bf16[512,1152]{1,0:T(8,128)(2,1)S(1)} %concatenate.37, bf16[1024,1664]{1,0:T(8,128)(2,1)} %bitcast.82), kind=kOutput, calls=%fused_computation.12 | convolution fusion | flops 1211628032 | bytes 5648384 | tf_op jit(solution)/shard_map/dot_general | solution.py:23
  138.0 0.7 concatenate.39
  138.7 1.7 convolution_convert_fusion
  140.4 0.9 convolution_convert_fusion.2
  141.3 2.0 pad_maximum_fusion
  143.3 3.0 %convolution_convert_fusion.1.out_ref = bf16[512,1024]{1,0:T(8,128)(2,1)} fusion(bf16[512,512]{1,0:T(8,128)(2,1)S(1)} %copy-done.21, bf16[1024,1664]{1,0:T(8,128)(2,1)} %bitcast.83), kind=kOutput, calls=%fused_computation.15 | convolution fusion | flops 537395200 | bytes 2621440 | tf_op jit(solution)/shard_map/dot_general | solution.py:23
  146.3 58.7 %closing_sums.1 = (f32[128,1024]{1,0:T(8,128)}, f32[128,64]{1,0:T(8,128)}, f32[128,8]{1,0:T(8,128)}, f32[128,512]{1,0:T(8,128)}, f32[512,256]{1,0:T(8,128)}, /*i...) custom-call(bf16[8,128,1664]{2,1,0:T(8,128)(2,1)} %bitcast.62, ...), custom_call_target="tpu_custom_call" | custom-call | tf_op jit(solution)/shard_map/closing_sums/pallas_call | solution.py:752
  205.1 0.8 bitcast_multiply_fusion
  205.9 2.4 %fusion.23 = (f32[512,256]{1,0:T(8,128)}, bf16[512,256]{1,0:T(8,128)(2,1)}) fusion(bf16[512,256]{1,0:T(8,128)(2,1)S(1)} %copy-done.1, bf16[512,256]{1,0:T(8,128)(2,1)S(1)} %copy-done.2, f32[512,256]{1,0:T(8,128)} %get-tuple-element.59, f32[512]{0:T(512)S(1)} %bitcast_multiply_fusion, f32[256]{0:T(256)S(1)} %bitcast.100, f32[512]{0:T(512)S(1)} %add_rsqrt_fusion.1, ...), kind=kLoop, calls=%fused_computation.33 | loop fusion | flops 1310720 | bytes 2366464 | tf_op jit(solution)/shard_map/add | solution.py:796
  208.2 1.2 reshape.144
  209.5 0.7 copy.117
  210.8 1.3 dynamic_slice.10
  212.1 0.7 copy.118
  212.7 0.7 reshape.146
  213.4 0.6 slice.145
  215.7 0.7 copy.128
  (94 shorter events, 6.9 us)
Async XLA Ops:
  59.8 3.7 %copy-start.9 = (s32[512]{0:T(512)S(1)}, s32[512]{0:T(512)}, u32[]{:S(2)}) copy-start(s32[512]{0:T(512)} %param.18) | copy-start | bytes 6148
  62.8 12.7 %copy-start.18 = (f32[8]{0:T(128)S(1)}, f32[8]{0:T(128)}, u32[]{:S(2)}) copy-start(f32[8]{0:T(128)} %param.28) | copy-start | bytes 100
  62.8 12.9 %copy-start.22 = (f32[8]{0:T(128)S(1)}, f32[8]{0:T(128)}, u32[]{:S(2)}) copy-start(f32[8]{0:T(128)} %param.29) | copy-start | bytes 100
  73.9 5.9 %copy-start.5 = (bf16[1024,1024]{1,0:T(8,128)(2,1)S(1)}, bf16[1024,1024]{1,0:T(8,128)(2,1)}, u32[]{:S(2)}) copy-start(bf16[1024,1024]{1,0:T(8,128)(2,1)} %get-tuple-element.41) | copy-start | bytes 6291460
  83.6 3.9 %copy-start.20 = (f32[8]{0:T(128)S(1)}, f32[8]{0:T(128)}, u32[]{:S(2)}) copy-start(f32[8]{0:T(128)} %param.30) | copy-start | bytes 100
  88.2 14.2 %copy-start.10 = (s32[512]{0:T(512)S(1)}, s32[512]{0:T(512)}, u32[]{:S(2)}) copy-start(s32[512]{0:T(512)} %param.18) | copy-start | bytes 6148
  117.4 1.8 copy-start
  117.4 2.2 %copy-start.13 = (f32[4,2,512]{2,1,0:T(2,128)S(1)}, f32[4,2,512]{2,1,0:T(2,128)}, u32[]{:S(2)}) copy-start(f32[4,2,512]{2,1,0:T(2,128)} %get-tuple-element.51) | copy-start | bytes 49156
  119.1 10.6 %copy-start.3 = (bf16[512,512]{1,0:T(8,128)(2,1)S(1)}, bf16[512,512]{1,0:T(8,128)(2,1)}, u32[]{:S(2)}) copy-start(bf16[512,512]{1,0:T(8,128)(2,1)} %get-tuple-element.46) | copy-start | bytes 1572868
  119.1 10.6 %copy-start.4 = (bf16[512,512]{1,0:T(8,128)(2,1)S(1)}, bf16[512,512]{1,0:T(8,128)(2,1)}, u32[]{:S(2)}) copy-start(bf16[512,512]{1,0:T(8,128)(2,1)} %get-tuple-element.47) | copy-start | bytes 1572868
  132.3 5.3 %copy-start.17 = (f32[4,64]{1,0:T(4,128)S(1)}, f32[4,64]{1,0:T(4,128)}, u32[]{:S(2)}) copy-start(f32[4,64]{1,0:T(4,128)} %get-tuple-element.56) | copy-start | bytes 3076
  132.3 5.4 %copy-start.16 = (f32[3,512]{1,0:T(4,128)S(1)}, f32[3,512]{1,0:T(4,128)}, u32[]{:S(2)}) copy-start(f32[3,512]{1,0:T(4,128)} %get-tuple-element.55) | copy-start | bytes 18436
  132.4 5.6 %copy-start.15 = (f32[4,512]{1,0:T(4,128)S(1)}, f32[4,512]{1,0:T(4,128)}, u32[]{:S(2)}) copy-start(f32[4,512]{1,0:T(4,128)} %get-tuple-element.54) | copy-start | bytes 24580
  132.4 5.6 %copy-start.19 = (f32[1,64]{1,0:T(1,128)S(1)}, f32[1,64]{1,0:T(1,128)}, u32[]{:S(2)}) copy-start(f32[1,64]{1,0:T(1,128)} %get-tuple-element.57) | copy-start | bytes 772
  132.4 6.3 %copy-start.6 = (bf16[1024,1024]{1,0:T(8,128)(2,1)S(1)}, bf16[1024,1024]{1,0:T(8,128)(2,1)}, u32[]{:S(2)}) copy-start(bf16[1024,1024]{1,0:T(8,128)(2,1)} %get-tuple-element.41) | copy-start | bytes 6291460
  138.7 1.7 copy-start.21
  146.3 59.6 %copy-start.1 = (bf16[512,256]{1,0:T(8,128)(2,1)S(1)}, bf16[512,256]{1,0:T(8,128)(2,1)}, u32[]{:S(2)}) copy-start(bf16[512,256]{1,0:T(8,128)(2,1)} %param.16) | copy-start | bytes 786436
  146.3 59.6 %copy-start.2 = (bf16[512,256]{1,0:T(8,128)(2,1)S(1)}, bf16[512,256]{1,0:T(8,128)(2,1)}, u32[]{:S(2)}) copy-start(bf16[512,256]{1,0:T(8,128)(2,1)} %param.17) | copy-start | bytes 786436
  205.1 3.2 %copy-start.7 = (f32[128,1024]{1,0:T(8,128)S(1)}, f32[128,1024]{1,0:T(8,128)}, u32[]{:S(2)}) copy-start(f32[128,1024]{1,0:T(8,128)} %get-tuple-element.62) | copy-start | bytes 1572868
  205.1 4.4 %copy-start.11 = (f32[128,64]{1,0:T(8,128)S(1)}, f32[128,64]{1,0:T(8,128)}, u32[]{:S(2)}) copy-start(f32[128,64]{1,0:T(8,128)} %get-tuple-element.116) | copy-start | bytes 98308
  205.1 5.1 %copy-start.14 = (f32[40,128]{1,0:T(8,128)S(1)}, f32[40,128]{1,0:T(8,128)}, u32[]{:S(2)}) copy-start(f32[40,128]{1,0:T(8,128)} %get-tuple-element.66) | copy-start | bytes 61444
  205.1 7.0 %copy-start.12 = (f32[128,8]{1,0:T(8,128)S(1)}, f32[128,8]{1,0:T(8,128)}, u32[]{:S(2)}) copy-start(f32[128,8]{1,0:T(8,128)} %get-tuple-element.117) | copy-start | bytes 12292
  205.1 10.6 %copy-start.8 = (f32[128,512]{1,0:T(8,128)S(1)}, f32[128,512]{1,0:T(8,128)}, u32[]{:S(2)}) copy-start(f32[128,512]{1,0:T(8,128)} %get-tuple-element.170) | copy-start | bytes 786436
where the time goes:
time: 217 us; the launch traced here: 216 us
  Pallas kernels  147 us (68%)
  local copies, waits for them, and re-layouts  31.6 us (15%)
  matrix products  20.6 us (9%)
  other arithmetic  10.7 us (5%)
  blocking collectives  5.96 us (3%)
    pallas_call x1, Pallas kernels, local(): pl.pallas_call(sum_kernel, in_specs=[vmem] * 5, out_specs=[vmem] * 9, out...  58.7 us
    pallas_call x1, Pallas kernels, local(): pl.pallas_call(gather_kernel, in_specs=[vmem, vmem], out_specs=[vmem, vme...  50.5 us
    pallas_call x1, Pallas kernels, local(): pl.pallas_call(backward_kernel, grid=(pairs,), in_specs=common_specs + [c...  13.3 us
    pallas_call x1, Pallas kernels, local(): pl.pallas_call(bc_back_kernel, out_shape=[shape((rows, bc_cols), BF16), s...  9.4 us
    dot_general x3, matrix products, plain_product(): lax.dot_general(left, right, (((1,), (0,)), ((), ())), preferred_element_...  8.64 us
    dot_general x2, matrix products, cols_product(): lax.dot_general(left, right, (((1,), (1,)), ((), ())), preferred_element_...  8.28 us
    pallas_call x1, Pallas kernels, local(): pl.pallas_call(forward_kernel, grid=(pairs,), in_specs=common_specs, out_...  7.52 us
    unnamed x56, local copies, waits for them, and re-layouts  6.44 us

commit v1 on v0

--- a/solution.py
+++ b/solution.py
@@ -1,4 +1,5 @@
 from functools import partial
+from types import SimpleNamespace
 
 import jax
 import jax.numpy as jnp
@@ -500,6 +501,1036 @@
     return jax.ShapeDtypeStruct(dims, dtype)
 
 
+def split_two(value):
+    high = value.astype(BF16).astype(F32)
+    return high, value - high
+
+
+def split_three(value):
+    high, rest = split_two(value)
+    middle, low = split_two(rest)
+    return high, middle, low
+
+
+class Spread:
+    def __init__(self, axis, own, slot, sems, own_sem):
+        self.axis, self.own, self.slot, self.sems, self.own_sem = axis, own, slot, sems, own_sem
+        self.me, self.high, self.low, self.highs, self.lows = lines(axis)
+
+    def index(self, high, low):
+        return high * self.lows + low
+
+    def has(self, way, steps):
+        if way == 0:
+            return self.high - steps >= 0
+        return self.high + steps < self.highs
+
+    def towards(self, way, steps):
+        return self.high - steps if way == 0 else self.high + steps
+
+    def keep(self):
+        return pltpu.make_async_copy(self.own, self.slot(self.me), self.own_sem)
+
+    def hop(self, way, step):
+        origin = self.index(self.towards(way, step - 1), self.low)
+        block = self.slot(origin)
+        onto = self.index(self.towards(1 - way, 1), self.low)
+        return remote(
+            self.own if step == 1 else block, block,
+            self.sems.at[0, way, step], self.sems.at[1, way, step], self.axis, onto,
+        )
+
+    def across(self, way, steps):
+        block = self.slot(self.index(self.towards(way, steps), self.low))
+        onto = self.index(self.high, 1 - self.low)
+        return remote(
+            self.own if steps == 0 else block, block,
+            self.sems.at[2, way, steps], self.sems.at[3, way, steps], self.axis, onto,
+        )
+
+    def sends(self, way, step):
+        return self.has(1 - way, 1) & self.has(way, step - 1)
+
+    def step(self, step):
+        if step >= self.highs:
+            return
+        if step == 0:
+            self.keep().start()
+        for way in range(2):
+            if step == 0:
+                pl.when(self.sends(way, 1))(lambda way=way: self.hop(way, 1).start())
+                continue
+
+            @pl.when(self.has(way, step))
+            def _(way=way):
+                self.hop(way, step).wait_recv()
+                if step + 1 < self.highs:
+                    pl.when(self.sends(way, step + 1))(lambda: self.hop(way, step + 1).start())
+                if self.lows == 2:
+                    self.across(way, step).start()
+
+        if step == 0 and self.lows == 2:
+            self.across(0, 0).start()
+
+    def finish(self):
+        self.keep().wait()
+        for step in range(1, self.highs):
+            for way in range(2):
+                pl.when(self.sends(way, step))(
+                    lambda way=way, step=step: self.hop(way, step).wait_send()
+                )
+        if self.lows == 2:
+            self.across(0, 0).wait()
+            for step in range(1, self.highs):
+                for way in range(2):
+                    pl.when(self.has(way, step))(
+                        lambda way=way, step=step: self.across(way, step).wait()
+                    )
+
+
+class Gradient:
+    def __init__(self, send, paired, held, landed, sems):
+        self.send, self.paired, self.held, self.landed, self.sems = send, paired, held, landed, sems
+        self.me, self.high, self.low, self.highs, self.lows = lines("dp")
+
+    def to(self, away):
+        return lax.rem(self.high + away, self.highs)
+
+    def theirs(self, away):
+        return self.to(away) * self.lows + (self.lows - 1 - self.low)
+
+    def mine(self, away):
+        return self.to(away) * self.lows + self.low
+
+    def cross(self, away):
+        partner = self.high * self.lows + (self.lows - 1 - self.low)
+        return remote(
+            self.send.at[self.theirs(away)], self.paired.at[away],
+            self.sems.at[0, away], self.sems.at[1, away], "dp", partner,
+        )
+
+    def going(self, away):
+        return remote(
+            self.held.at[away], self.landed.at[away],
+            self.sems.at[2, away], self.sems.at[3, away], "dp", self.mine(away),
+        )
+
+    def fill(self, away, make):
+        if self.lows == 2:
+            theirs = self.theirs(away)
+            self.send[theirs] = make(theirs)
+            self.cross(away).start()
+        mine = self.mine(away)
+        self.send[mine] = make(mine)
+
+    def both(self, away):
+        both = self.send[self.mine(away)].astype(F32)
+        if self.lows == 2:
+            self.cross(away).wait()
+            both = both + self.paired[away].astype(F32)
+        return both
+
+    def relay(self, away):
+        self.held[away] = self.both(away).astype(BF16)
+        self.going(away).start()
+
+    def result(self, order):
+        total = self.both(0)
+        for away in order[:-1]:
+            self.going(away).wait()
+            total = total + self.landed[away].astype(F32)
+        return total
+
+
+def silu_parts(value):
+    logistic = jax.nn.sigmoid(value)
+    return logistic, value * logistic
+
+
+def layer_kernel(
+    zx_ref, x_ref, cot_ref, wo_ref, wbc_in, wdt_in, norm_in, seq_in,
+    taps_in, bias_in, bct_in, bcb_in, dtb_in, alog_in, skip_in, gain_in,
+    out_ref, grad_ref, gzx_ref, gside_ref, gwo_ref, gnorm_ref, gtaps_ref, gbias_ref, ggate_ref,
+    gbct_ref, gbcb_ref, gdtb_ref, galog_ref, gskip_ref,
+    scratch,
+):
+    s = SimpleNamespace(**scratch)
+    fetched = (
+        (wbc_in, s.wbc_in), (wdt_in, s.wdt_in), (norm_in, s.norm_in), (seq_in, s.seq_in),
+        (taps_in, s.taps_in), (bias_in, s.bias_in), (bct_in, s.bct_in), (bcb_in, s.bcb_in),
+        (dtb_in, s.dtb_in), (alog_in, s.alog_in), (skip_in, s.skip_in), (gain_in, s.gain_in),
+    )
+    fetches = [
+        pltpu.make_async_copy(source, target, s.fetch_sems.at[k])
+        for k, (source, target) in enumerate(fetched)
+    ]
+    for copy in fetches:
+        copy.start()
+    (
+        wbc_ref, wdt_ref, norm_ref, seq_ref, taps_ref, bias_ref, bct_ref, bcb_ref, dtb_ref,
+        alog_ref, skip_ref, gain_ref,
+    ) = [target for _, target in fetched]
+    rows, share = x_ref.shape
+    inner = wo_ref.shape[1]
+    side_rows, held = s.sideown.shape
+    taps = taps_ref.shape[0]
+    heads = skip_ref.shape[1]
+    bc_cols = bct_ref.shape[1]
+    tile = 128
+    pairs = inner // tile
+    chunks = rows // tile
+    per_tile = tile // HEAD_DIM
+    width = s.xr.shape[1]
+    blocks = width // held
+    state = s.bm.shape[1]
+    gain_at = bc_cols + heads
+    tensor_count = lax.axis_size("tensor")
+    tensor_me = lax.axis_index("tensor")
+    inner_all = inner * tensor_count
+
+    def at(index, size=tile):
+        return pl.ds(pl.multiple_of(index * size, size), size)
+
+    def lanes(p):
+        return slice(p * tile, (p + 1) * tile)
+
+    def each_chunk(body):
+        def step(c, carry):
+            body(c, at(c))
+            return carry
+
+        lax.fori_loop(0, chunks, step, 0)
+
+    def share_of(ref):
+        return lambda index: ref.at[:, at(index, share)]
+
+    def block_of(ref):
+        return lambda index: ref.at[index]
+
+    own_sems = s.own_sems
+    xs = Spread("tensor", x_ref, share_of(s.xr), s.xs_sems, own_sems.at[0])
+    cs = Spread("tensor", cot_ref, share_of(s.cr), s.cs_sems, own_sems.at[1])
+    side = Spread("dp", s.sideown, block_of(s.side), s.side_sems, own_sems.at[2])
+    wx = Spread("dp", zx_ref.at[:, inner:], block_of(s.wx), s.wx_sems, own_sems.at[3])
+    wz = Spread("dp", zx_ref.at[:, :inner], block_of(s.wz), s.wz_sems, own_sems.at[4])
+    wo = Spread("dp", wo_ref, block_of(s.wo), s.wo_sems, own_sems.at[5])
+    highs = wx.highs
+    order = list(range(highs - 1, -1, -1))
+
+    def peers(ref, slots, sems, base=0):
+        return [
+            remote(
+                ref, slots.at[away - 1], sems.at[0, base + away], sems.at[1, base + away],
+                "tensor", lax.rem(tensor_me + away, tensor_count),
+            )
+            for away in range(1, tensor_count)
+        ]
+
+    greet_all(pltpu.get_barrier_semaphore())
+    xs.step(0)
+    wx.step(0)
+    for copy in fetches:
+        copy.wait()
+    s.sideown[...] = jnp.concatenate(
+        [
+            wbc_ref[...].astype(F32), wdt_ref[...].astype(F32), norm_ref[...].astype(F32),
+            jnp.zeros((side_rows - gain_at - 1, held), F32),
+        ],
+        axis=0,
+    ).astype(BF16)
+    side.step(0)
+    cs.step(0)
+
+    s.cols[...] = jnp.zeros_like(s.cols)
+    s.cols[:taps, :bc_cols] = bct_ref[...]
+    s.cols[taps : taps + 1, :bc_cols] = bcb_ref[...]
+    s.cols[0:1, bc_cols:gain_at] = dtb_ref[...]
+    s.cols[1:2, bc_cols:gain_at] = alog_ref[...]
+    s.cols[...] = s.cols[...].T
+    seq = seq_ref[...].astype(F32)
+    at_lane = lax.broadcasted_iota(jnp.int32, (1, rows), 1)
+    seq_wide = jnp.broadcast_to(seq, (tile, rows)).T
+    s.seg[...] = seq_wide
+    row_at = lax.broadcasted_iota(jnp.int32, (rows, tile), 0)
+    for shift in range(1, taps):
+        same = (pltpu.roll(seq_wide, shift, 0) == seq_wide) & (row_at >= shift)
+        s.mask[shift - 1] = same.astype(F32)
+    lane_masks = [None] + [
+        ((pltpu.roll(seq, shift, 1) == seq) & (at_lane >= shift)).astype(F32)
+        for shift in range(1, taps)
+    ]
+    live = (seq >= 0).astype(F32)
+
+    def link_rows(c, held_rows):
+        seg = s.seg[held_rows]
+        for k in range(chunks):
+            down = lax.broadcasted_iota(jnp.int32, (tile, tile), 0) + c * tile
+            right = lax.broadcasted_iota(jnp.int32, (tile, tile), 1) + k * tile
+            joined = (seg == seq[:, lanes(k)]) & (down >= right)
+            s.link[held_rows, lanes(k)] = joined.astype(F32).astype(BF16)
+
+    each_chunk(link_rows)
+    side.step(1)
+    wx.step(1)
+    xs.step(1)
+    side.step(2)
+    wx.step(2)
+    xs.finish()
+
+    def norm_rows(c, held_rows):
+        squares = jnp.zeros((tile, tile), F32)
+        for k in range(width // tile):
+            part = s.xr[held_rows, lanes(k)].astype(F32)
+            squares = squares + part * part
+        mean = jnp.sum(squares, axis=1, keepdims=True) / width
+        s.inv[held_rows] = jnp.broadcast_to(lax.rsqrt(mean + EPSILON), (tile, tile))
+
+    each_chunk(norm_rows)
+    wz.step(0)
+    side.step(3)
+    wx.step(3)
+    side.finish()
+    cs.step(1)
+    wo.step(0)
+    for step in range(4, highs):
+        side.step(step)
+        wx.step(step)
+
+    def gain_row(k):
+        return s.side[k, gain_at : gain_at + 1, :].astype(F32)
+
+    def normed_rows(c, held_rows):
+        for k in range(blocks):
+            here = slice(k * held, (k + 1) * held)
+            inv = jnp.concatenate([s.inv[held_rows]] * (held // tile), axis=1)
+            value = s.xr[held_rows, here].astype(F32) * inv * gain_row(k)
+            s.normed[held_rows, here] = value.astype(BF16)
+
+    each_chunk(normed_rows)
+    side_all = jnp.concatenate([s.side[k] for k in range(blocks)], axis=1)
+    side_pre = cols_product(side_all, s.normed[...])
+    bc_pre = side_pre[:bc_cols].astype(BF16).astype(F32)
+    s.bcpre[...] = bc_pre
+
+    def bc_taps(k):
+        return s.cols[:bc_cols, k : k + 1]
+
+    def bc_value(source):
+        value = bc_taps(taps) + bc_taps(taps - 1) * source
+        for shift in range(1, taps):
+            value = value + bc_taps(taps - 1 - shift) * (
+                pltpu.roll(source, shift, 1) * lane_masks[shift]
+            )
+        return value
+
+    value = bc_value(bc_pre)
+    s.bcown[...] = silu_parts(value)[1].astype(BF16)
+    bc_copies = [
+        remote(
+            s.bcown, s.bct.at[tensor_me], s.bc_sems.at[0, away], s.bc_sems.at[1, away],
+            "tensor", lax.rem(tensor_me + away, tensor_count),
+        )
+        for away in range(1, tensor_count)
+    ]
+    for copy in bc_copies:
+        copy.start()
+    s.bct[tensor_me] = s.bcown[...]
+
+    dt_in = side_pre[bc_cols:gain_at] + s.cols[bc_cols:gain_at, 0:1]
+    rate = -jnp.exp(s.cols[bc_cols:gain_at, 1:2])
+    step_size = jnp.maximum(dt_in, 0.0) + jnp.log1p(jnp.exp(-jnp.abs(dt_in)))
+    log_decay = step_size * rate
+    s.dtin[...] = dt_in
+    s.ld[...] = log_decay
+    zeros = jnp.zeros((heads, rows), F32)
+    stacked = jnp.concatenate(split_three(log_decay) + (zeros,), axis=0).astype(BF16)
+    summed = cols_product(stacked, s.link[...])
+    cum = summed[:heads] + summed[heads : 2 * heads] + summed[2 * heads : 3 * heads]
+    s.cum[...] = cum
+    entry, tail = [], []
+    for c in range(chunks):
+        here = slice(c * tile, (c + 1) * tile)
+        last = slice((c + 1) * tile - 1, (c + 1) * tile)
+        if c == 0:
+            entry.append(jnp.zeros((heads, tile), F32))
+        else:
+            before = slice(c * tile - 1, c * tile)
+            joined = (seq[:, here] == seq[:, before]).astype(F32)
+            entry.append(jnp.exp(jnp.minimum(cum[:, here] - cum[:, before], 0.0)) * joined)
+        joined = (seq[:, here] == seq[:, last]).astype(F32)
+        tail.append(jnp.exp(jnp.minimum(cum[:, last] - cum[:, here], 0.0)) * joined)
+    parts = (cum,)
+    for value in (step_size, jnp.concatenate(entry, axis=1), jnp.concatenate(tail, axis=1)):
+        parts = parts + split_two(value)
+    spare = jnp.zeros((tile - len(parts) * heads, rows), F32)
+    columns = jnp.concatenate(parts + (spare,), axis=0).T
+    s.cumc[...] = columns
+    columns = columns.astype(BF16)
+    row_id = lax.broadcasted_iota(jnp.int32, (tile, inner), 0)
+    head_id = lax.broadcasted_iota(jnp.int32, (tile, inner), 1) // HEAD_DIM
+    for k, spread in enumerate((s.stepw, s.entw, s.tailw)):
+        first = heads * (1 + 2 * k)
+        pick = (row_id == head_id + first) | (row_id == head_id + first + heads)
+        spread[...] = plain_product(columns, pick.astype(F32).astype(BF16))
+
+    wx.finish()
+
+    def x_rows(c, held_rows):
+        weight = s.wx[...].reshape(width, inner)
+        value = plain_product(s.normed[held_rows], weight)
+        s.xpre[held_rows] = value.astype(BF16).astype(F32)
+
+    each_chunk(x_rows)
+    wz.step(1)
+
+    def mask(shift):
+        return s.mask[shift - 1]
+
+    for p in range(pairs):
+        here = lanes(p)
+        source = s.xpre[:, here]
+        value = bias_ref[:, here] + taps_ref[taps - 1 : taps, here] * source
+        for shift in range(1, taps):
+            value = value + taps_ref[taps - 1 - shift : taps - shift, here] * (
+                pltpu.roll(source, shift, 0) * mask(shift)
+            )
+        s.val[:, here] = value
+        act = silu_parts(value)[1].astype(BF16).astype(F32)
+        s.act[:, here] = act
+        stepped = act * s.stepw[:, here]
+        s.vb[:, here] = stepped.astype(BF16)
+        s.xt[:, here] = (stepped * s.tailw[:, here]).astype(BF16)
+
+    wz.step(2)
+    cs.finish()
+    for copy in bc_copies:
+        copy.wait()
+    halfway = tensor_count // 2
+    bt = s.bct[:halfway].reshape(state, rows)
+    ct = s.bct[halfway:].reshape(state, rows)
+    s.bm[...] = bt.astype(F32).T.astype(BF16)
+    s.cm[...] = ct.astype(F32).T.astype(BF16)
+    wz.step(3)
+    for step in range(4, highs):
+        wz.step(step)
+    wo.step(1)
+
+    first_head = lax.broadcasted_iota(jnp.int32, (tile, tile), 1) < HEAD_DIM
+
+    def two_parts(value):
+        blank = jnp.zeros_like(value)
+        return jnp.concatenate(
+            [jnp.where(first_head, value, blank), jnp.where(first_head, blank, value)], axis=0
+        )
+
+    s.state[...] = jnp.zeros_like(s.state)
+
+    def scan_rows(c, held_rows):
+        here = at(c)
+        c_rows, b_rows = s.cm[held_rows], s.bm[held_rows]
+        scores = cols_product(c_rows, b_rows) * s.link[held_rows, here].astype(F32)
+        prior = s.state[...].astype(BF16)
+        s.prior[c] = prior
+        carried = plain_product(c_rows, prior) * s.entw[held_rows]
+        for p in range(pairs):
+            wide = []
+            for head in range(per_tile):
+                h = p * per_tile + head
+                spread = s.cumc[held_rows, h : h + 1] - s.cum[h : h + 1, here]
+                decay = jnp.exp(jnp.minimum(spread, 0.0))
+                s.decay[c, p, :, head * tile : (head + 1) * tile] = decay
+                wide.append((scores * decay).astype(BF16))
+            s.wst[c, p] = jnp.concatenate(wide, axis=0)
+            both = two_parts(s.vb[held_rows, lanes(p)].astype(F32)).astype(BF16)
+            inside = plain_product(jnp.concatenate(wide, axis=1), both)
+            s.ynos[held_rows, lanes(p)] = inside + carried[:, lanes(p)]
+        last = s.entw[pl.ds(c * tile + tile - 1, 1)]
+        s.state[...] = s.state[...] * last + rows_product(b_rows, s.xt[held_rows])
+
+    each_chunk(scan_rows)
+    skip_wide = jnp.concatenate(
+        [jnp.broadcast_to(skip_ref[:, h : h + 1], (1, HEAD_DIM)) for h in range(heads)], axis=1
+    )
+    wz.finish()
+    wo.step(2)
+
+    def gate_rows(c, held_rows):
+        z = plain_product(s.normed[held_rows], s.wz[...].reshape(width, inner))
+        squares = jnp.zeros((tile, tile), F32)
+        for p in range(pairs):
+            here = lanes(p)
+            z_part = z[:, here].astype(BF16).astype(F32)
+            s.z[held_rows, here] = z_part
+            y = s.ynos[held_rows, here] + skip_wide[:, here] * s.act[held_rows, here]
+            gated = y * silu_parts(z_part)[1]
+            s.gated[held_rows, here] = gated
+            s.q[held_rows, here] = (gated * gain_ref[:, here]).astype(BF16)
+            squares = squares + gated * gated
+        s.wide[held_rows] = squares
+
+    each_chunk(gate_rows)
+
+    def as_row(ref):
+        return jnp.sum(ref[...].T, axis=0, keepdims=True)
+
+    s.stat[0] = jnp.broadcast_to(as_row(s.wide), (8, rows))
+    stat_copies = peers(s.stat.at[0], s.stat_slots.at[0], s.stat_sems)
+    for copy in stat_copies:
+        copy.start()
+    wo.step(3)
+    for step in range(4, highs):
+        wo.step(step)
+
+    def turn(k, carry):
+        here = at(k)
+        s.nt[here] = s.normed[:, here].astype(F32).T.astype(BF16)
+        s.ct[here] = s.cr[:, here].astype(F32).T.astype(BF16)
+        return carry
+
+    lax.fori_loop(0, width // tile, turn, 0)
+
+    def collect(copies, which):
+        total = s.stat[which]
+        for away, copy in enumerate(copies):
+            copy.wait()
+            total = total + s.stat_slots[which, away]
+        return total[0:1]
+
+    squares = collect(stat_copies, 0)
+    inv_gate = lax.rsqrt(squares / inner_all + EPSILON)
+    row_scale = inv_gate * live
+    s.rs[...] = jnp.broadcast_to(row_scale, (tile, rows)).T
+
+    go = Gradient(s.go_send, s.go_pair, s.go_held, s.go_land, s.go_sems)
+    gz = Gradient(s.gz_send, s.gz_pair, s.gz_held, s.gz_land, s.gz_sems)
+    gx = Gradient(s.gx_send, s.gx_pair, s.gx_held, s.gx_land, s.gx_sems)
+    gs = Gradient(s.gs_send, s.gs_pair, s.gs_held, s.gs_land, s.gs_sems)
+
+    def out_block(k):
+        scaled = (s.ct[at(k, held)].astype(F32) * row_scale).astype(BF16)
+        return plain_product(scaled, s.q[...]).astype(BF16)
+
+    for away in order:
+        go.fill(away, out_block)
+
+    wo.finish()
+
+    def dq_rows(c, held_rows):
+        dq = plain_product(s.cr[held_rows], s.wo[...].reshape(width, inner))
+        total = jnp.zeros((tile, tile), F32)
+        for p in range(pairs):
+            here = lanes(p)
+            s.dq[held_rows, here] = dq[:, here]
+            total = total + s.q[held_rows, here].astype(F32) * dq[:, here]
+        s.wide[held_rows] = total
+
+    each_chunk(dq_rows)
+    s.stat[1] = jnp.broadcast_to(as_row(s.wide), (8, rows))
+    stat_copies = peers(s.stat.at[1], s.stat_slots.at[1], s.stat_sems, tensor_count)
+    for copy in stat_copies:
+        copy.start()
+
+    def out_part(index):
+        weight = s.wo[...].reshape(width, inner)
+        del weight
+        return cols_product(s.q[...], wo_rows(index))
+
+    def wo_rows(index):
+        per = share // held
+        return jnp.concatenate([s.wo[index * per + k] for k in range(per)], axis=0)
+
+    def wx_rows(ref, index):
+        per = share // held
+        return jnp.concatenate([ref[index * per + k] for k in range(per)], axis=0)
+
+    out_parts = (s.op_send, s.op_slots, s.op_sems)
+    norm_parts = (s.np_send, s.np_slots, s.np_sems)
+
+    def part_copy(parts, away):
+        send, slots, sems = parts
+        return remote(
+            send.at[away], slots.at[away - 1], sems.at[0, away], sems.at[1, away],
+            "tensor", lax.rem(tensor_me + away, tensor_count),
+        )
+
+    turns = sorted(range(1, tensor_count), key=lambda k: k % 2)
+    for away in turns:
+        s.op_send[away] = out_part(lax.rem(tensor_me + away, tensor_count)).astype(BF16)
+        part_copy(out_parts, away).start()
+    s.op_own[...] = out_part(tensor_me)
+
+    inner_dot = collect(stat_copies, 1)
+    pull = inv_gate * inv_gate * (inner_dot * row_scale) / inner_all
+    s.pull[...] = jnp.broadcast_to(pull, (tile, rows)).T
+    s.sums[...] = jnp.zeros_like(s.sums)
+
+    def slope_rows(c, held_rows):
+        scale, pulled = s.rs[held_rows], s.pull[held_rows]
+        for p in range(pairs):
+            here = lanes(p)
+            z = s.z[held_rows, here]
+            gated = s.gated[held_rows, here]
+            act = s.act[held_rows, here]
+            logistic, z_silu = silu_parts(z)
+            y = s.ynos[held_rows, here] + skip_wide[:, here] * act
+            dq = s.dq[held_rows, here] * scale
+            d_gated = dq * gain_ref[:, here] - gated * pulled
+            d_y = d_gated * z_silu
+            d_z = d_gated * y * (logistic * (1.0 + z * (1.0 - logistic)))
+            s.dz[held_rows, here] = d_z.astype(BF16)
+            s.dy[held_rows, here] = d_y
+            s.edy[held_rows, here] = (d_y * s.entw[held_rows, here]).astype(BF16)
+            s.sums[5:6, here] += jnp.sum(dq * gated, axis=0, keepdims=True)
+            s.sums[6:7, here] += jnp.sum(d_y * act, axis=0, keepdims=True)
+
+    each_chunk(slope_rows)
+    go.relay(order[0])
+
+    def z_block(k):
+        return plain_product(s.nt[at(k, held)], s.dz[...]).astype(BF16)
+
+    for away in order:
+        gz.fill(away, z_block)
+        if away != order[0] and away != 0:
+            go.relay(away)
+
+    s.state[...] = jnp.zeros_like(s.state)
+
+    def back_rows(turn, held_rows):
+        c = chunks - 1 - turn
+        held_rows = at(c)
+        c_rows, b_rows = s.cm[held_rows], s.bm[held_rows]
+        later = s.state[...].astype(BF16)
+        edy = s.edy[held_rows]
+        carried = plain_product(b_rows, later) * s.tailw[held_rows]
+        s.dvc[held_rows] = carried
+        d_scores = jnp.zeros((tile, tile), F32)
+        for p in range(pairs):
+            here = lanes(p)
+            dy_rows = s.dy[held_rows, here].astype(BF16)
+            v_both = two_parts(s.vb[held_rows, here].astype(F32)).astype(BF16)
+            d_weights = cols_product(dy_rows, v_both) * s.decay[c, p]
+            for head in range(per_tile):
+                d_scores = d_scores + d_weights[:, head * tile : (head + 1) * tile]
+            dy_both = two_parts(dy_rows.astype(F32)).astype(BF16)
+            inside = rows_product(s.wst[c, p], dy_both)
+            s.dv[held_rows, here] = inside
+        d_scores = (d_scores * s.link[held_rows, held_rows].astype(F32)).astype(BF16)
+        s.dbc[:state, held_rows] = rows_product(c_rows, d_scores) + cols_product(
+            later, s.xt[held_rows]
+        )
+        s.dbc[state:, held_rows] = lax.dot_general(
+            b_rows, d_scores, (((0,), (1,)), ((), ())), preferred_element_type=F32
+        ) + cols_product(s.prior[c], edy)
+        last = s.entw[pl.ds(c * tile + tile - 1, 1)]
+        kept = s.state[...] * last
+        through = jnp.sum(kept * s.prior[c].astype(F32), axis=0, keepdims=True)
+        s.through[c] = jnp.broadcast_to(through, (8, inner))
+        s.state[...] = kept + rows_product(c_rows, edy)
+
+    each_chunk(back_rows)
+    for index in range(tensor_count):
+        s.dbc_send[index] = s.dbc[index * bc_cols : (index + 1) * bc_cols].astype(BF16)
+    dbc_copies = [
+        remote(
+            s.dbc_send.at[lax.rem(tensor_me + away, tensor_count)],
+            s.dbc_slots.at[away - 1], s.dbc_sems.at[0, away], s.dbc_sems.at[1, away],
+            "tensor", lax.rem(tensor_me + away, tensor_count),
+        )
+        for away in range(1, tensor_count)
+    ]
+    for copy in dbc_copies:
+        copy.start()
+
+    head_row = lax.broadcasted_iota(jnp.int32, (8 * -(-heads // 8), tile), 0)
+    head_lane = lax.broadcasted_iota(jnp.int32, (8 * -(-heads // 8), tile), 1) // HEAD_DIM
+    d_step, d_cum, d_tail, passed = zeros, zeros, zeros, jnp.zeros((heads, 8 * chunks), F32)
+    for p in range(pairs):
+        here = lanes(p)
+        act, d_inside, d_carried = s.act[:, here], s.dv[:, here], s.dvc[:, here]
+        d_v = d_inside + d_carried
+        v_part = s.vb[:, here].astype(F32)
+        d_y = s.dy[:, here]
+        step_wide = s.stepw[:, here]
+        pick = (head_row == head_lane + p * per_tile).astype(F32).astype(BF16)
+        direct = d_v * act
+        turned = d_y.astype(BF16).astype(F32) * s.ynos[:, here] - v_part * d_inside
+        through = jnp.concatenate([s.through[c, :, here] for c in range(chunks)], axis=0)
+        for part in split_two(direct):
+            d_step = d_step + cols_product(pick, part.astype(BF16))
+        for part in split_three(turned):
+            d_cum = d_cum + cols_product(pick, part.astype(BF16))
+        for part in split_two(v_part * d_carried):
+            d_tail = d_tail + cols_product(pick, part.astype(BF16))
+        for part in split_two(through):
+            passed = passed + cols_product(pick, part.astype(BF16))
+        d_act = d_v * step_wide + skip_wide[:, here] * d_y
+        source = s.xpre[:, here]
+        value = s.val[:, here]
+        logistic = jax.nn.sigmoid(value)
+        d_value = d_act * (logistic * (1.0 + value * (1.0 - logistic)))
+        d_source = taps_ref[taps - 1 : taps, here] * d_value
+        s.sums[taps - 1 : taps, here] = jnp.sum(d_value * source, axis=0, keepdims=True)
+        s.sums[taps : taps + 1, here] = jnp.sum(d_value, axis=0, keepdims=True)
+        for shift in range(1, taps):
+            kept = d_value * mask(shift)
+            s.sums[taps - 1 - shift : taps - shift, here] = jnp.sum(
+                kept * pltpu.roll(source, shift, 0), axis=0, keepdims=True
+            )
+            d_source = d_source + taps_ref[taps - 1 - shift : taps - shift, here] * pltpu.roll(
+                kept, rows - shift, 0
+            )
+        s.dx[:, here] = d_source.astype(BF16)
+
+    def x_block(k):
+        return plain_product(s.nt[at(k, held)], s.dx[...]).astype(BF16)
+
+    gz.relay(order[0])
+    for away in order[:2]:
+        gx.fill(away, x_block)
+    gz.relay(order[1])
+
+    wide = s.dbc_send[tensor_me].astype(F32)
+    for away, copy in enumerate(dbc_copies):
+        copy.wait()
+        wide = wide + s.dbc_slots[away].astype(F32)
+    source = s.bcpre[...]
+    value = bc_value(source)
+    logistic = jax.nn.sigmoid(value)
+    d_value = wide * (logistic * (1.0 + value * (1.0 - logistic)))
+    d_source = bc_taps(taps - 1) * d_value
+    tap_cols = {taps - 1: d_value * source, taps: d_value}
+    for shift in range(1, taps):
+        kept = d_value * lane_masks[shift]
+        tap_cols[taps - 1 - shift] = kept * pltpu.roll(source, shift, 1)
+        d_source = d_source + bc_taps(taps - 1 - shift) * pltpu.roll(kept, rows - shift, 1)
+
+    decays = []
+    blank = jnp.zeros((heads, tile), F32)
+    for c in range(chunks):
+        linked = s.link[lanes(c), lanes(c)]
+        ahead, behind = d_cum[:, lanes(c)], d_tail[:, lanes(c)]
+        total = passed[:, 8 * c : 8 * c + 1] - behind
+        for value, product in ((ahead, plain_product), (behind, cols_product)):
+            stacked = jnp.concatenate(split_three(value) + (blank,), axis=0).astype(BF16)
+            summed = product(stacked, linked)
+            total = total + summed[:heads] + summed[heads : 2 * heads]
+            total = total + summed[2 * heads : 3 * heads]
+        decays.append(total)
+    d_decay = jnp.concatenate(decays, axis=1)
+    d_dt = (d_step[:heads] + d_decay * rate) * jax.nn.sigmoid(s.dtin[...])
+    d_side = jnp.concatenate(
+        [d_source, d_dt, jnp.zeros((side_rows - gain_at, rows), F32)], axis=0
+    ).astype(BF16)
+    s.dside[...] = d_side
+
+    def side_block(k):
+        return cols_product(s.dside[...], s.nt[at(k, held)]).astype(BF16)
+
+    for away in order:
+        gs.fill(away, side_block)
+    for away in order[2:-1]:
+        gx.fill(away, x_block)
+        gz.relay(away)
+    gx.fill(0, x_block)
+
+    def placed(columns, height):
+        lane = lax.broadcasted_iota(jnp.int32, (height, tile), 1)
+        total = jnp.zeros((height, tile), F32)
+        for k, column in columns.items():
+            total = total + jnp.where(lane == k, jnp.sum(column, axis=1, keepdims=True), 0.0)
+        return total
+
+    small = jnp.concatenate(
+        [
+            placed(tap_cols, bc_cols),
+            placed({0: d_dt, 1: d_decay * s.ld[...]}, heads),
+            jnp.zeros((tile - gain_at, tile), F32),
+        ],
+        axis=0,
+    ).T
+    s.sums[8:16, :tile] = small[:8]
+
+    s.meanw[...] = jnp.zeros_like(s.meanw)
+    per = share // held
+
+    def norm_part(index):
+        total = cols_product(s.dz[...], wx_rows(s.wz, index))
+        total = total + cols_product(s.dx[...], wx_rows(s.wx, index))
+        sides = jnp.concatenate([s.side[index * per + k] for k in range(per)], axis=1)
+        total = total + rows_product(s.dside[...], sides)
+        here = at(index, share)
+        inv = jnp.concatenate([s.inv[...]] * (share // tile), axis=1)
+        weighed = total * (s.xr[:, here].astype(F32) * inv)
+        gains = [gain_row(index * per + k) for k in range(per)]
+        for k in range(per):
+            s.gpart[index * per + k] = jnp.broadcast_to(
+                jnp.sum(weighed[:, k * held : (k + 1) * held], axis=0, keepdims=True), (8, held)
+            )
+        rated = weighed * jnp.concatenate(gains, axis=1)
+        for k in range(share // tile):
+            s.meanw[...] += rated[:, lanes(k)]
+        return total
+
+    for away in turns:
+        s.np_send[away] = norm_part(lax.rem(tensor_me + away, tensor_count)).astype(BF16)
+        part_copy(norm_parts, away).start()
+    s.np_own[...] = norm_part(tensor_me)
+    s.stat[2] = jnp.broadcast_to(as_row(s.meanw), (8, rows))
+    stat_copies = peers(s.stat.at[2], s.stat_slots.at[2], s.stat_sems, 2 * tensor_count)
+    for copy in stat_copies:
+        copy.start()
+    s.sums[8:16, tile : tile + held] = jnp.concatenate(
+        [s.gpart[k, 0:1] for k in range(blocks)], axis=0
+    )
+    pair_copy = remote(
+        s.sums, s.sum_pair, s.sum_sems.at[0, 0], s.sum_sems.at[1, 0], "dp",
+        gx.high * gx.lows + (gx.lows - 1 - gx.low),
+    )
+    if gx.lows == 2:
+        pair_copy.start()
+    for away in order[:2]:
+        gx.relay(away)
+    if gx.lows == 2:
+        pair_copy.wait()
+        s.sums_two[...] = s.sums[...] + s.sum_pair[...]
+    else:
+        s.sums_two[...] = s.sums[...]
+    small_copies = [
+        remote(
+            s.sums_two, s.sum_slots.at[away - 1], s.sum_sems.at[0, away],
+            s.sum_sems.at[1, away], "dp", gx.mine(away),
+        )
+        for away in range(1, highs)
+    ]
+    for copy in small_copies:
+        copy.start()
+    for away in order[:-1]:
+        gs.relay(away)
+    for away in order[2:-1]:
+        gx.relay(away)
+
+    gwo_ref[...] = go.result(order)
+    total = s.op_own[...]
+    for away in range(1, tensor_count):
+        part_copy(out_parts, away).wait()
+        total = total + s.op_slots[away - 1].astype(F32)
+    scale = jnp.concatenate([s.rs[...]] * (share // tile), axis=1)
+    here = at(tensor_me, share)
+    x_own = s.xr[:, here].astype(F32)
+    out_ref[...] = (x_own + total * scale).astype(BF16)
+    gzx_ref[:, :inner] = gz.result(order)
+
+    for copy in small_copies:
+        copy.wait()
+    total = s.sums_two[...]
+    for away in range(1, highs):
+        total = total + s.sum_slots[away - 1]
+    gtaps_ref[...] = total[:taps]
+    gbias_ref[...] = total[taps : taps + 1]
+    ggate_ref[...] = total[5:6]
+    gbct_ref[...] = total[8 : 8 + taps, :bc_cols]
+    gbcb_ref[...] = total[8 + taps : 9 + taps, :bc_cols]
+    gdtb_ref[...] = total[8:9, bc_cols:gain_at]
+    galog_ref[...] = total[9:10, bc_cols:gain_at]
+    lane = lax.broadcasted_iota(jnp.int32, (1, heads), 1)
+    skips = jnp.zeros((1, heads), F32)
+    for h in range(heads):
+        part = jnp.sum(total[6:7, h * HEAD_DIM : (h + 1) * HEAD_DIM], axis=1, keepdims=True)
+        skips = skips + jnp.where(lane == h, part, 0.0)
+    gskip_ref[...] = skips
+    s.gsum[...] = total[8:16, tile : tile + held]
+    gain_copies = peers(s.gsum, s.gain_slots, s.gain_sems)
+    for copy in gain_copies:
+        copy.start()
+
+    mean = collect(stat_copies, 2) / width
+    mean_wide = jnp.broadcast_to(mean, (tile, rows)).T
+    total = s.np_own[...]
+    for away in range(1, tensor_count):
+        part_copy(norm_parts, away).wait()
+        total = total + s.np_slots[away - 1].astype(F32)
+    own_gain = jnp.concatenate([gain_row(tensor_me * per + k) for k in range(per)], axis=1)
+    inv = s.inv[...]
+    pulled = jnp.concatenate([inv * mean_wide] * (share // tile), axis=1)
+    inv = jnp.concatenate([inv] * (share // tile), axis=1)
+    grad_ref[...] = inv * (total * own_gain - x_own * pulled) + s.cr[:, here].astype(F32)
+    gains = s.gsum[...]
+    for away, copy in enumerate(gain_copies):
+        copy.wait()
+        gains = gains + s.gain_slots[away]
+    row = lax.broadcasted_iota(jnp.int32, gains.shape, 0)
+    gnorm_ref[...] = jnp.sum(
+        jnp.where(row == lax.axis_index("dp"), gains, 0.0), axis=0, keepdims=True
+    )
+    gside_ref[...] = gs.result(order)
+    gzx_ref[:, inner:] = gx.result(order)
+
+
+def finish_kernel(
+    out_in, grad_in, gzx_in, gside_in, gwo_in, gnorm_in, gtaps_in, gbias_in, ggate_in,
+    gbct_in, gbcb_in, gdtb_in, galog_in, gskip_in,
+    out_ref, grad_ref, gzx_ref, gbc_ref, gdt_ref, gwo_ref, gnorm_ref, gtaps_ref, gbias_ref,
+    ggate_ref, gbct_ref, gbcb_ref, gdtb_ref, galog_ref, gskip_ref,
+    zx, sems,
+):
+    bc_cols, heads, inner = gbc_ref.shape[0], gdt_ref.shape[0], zx.shape[2]
+    moves = (
+        (out_in, out_ref), (grad_in, grad_ref), (gwo_in, gwo_ref),
+        (gside_in.at[:bc_cols], gbc_ref), (gside_in.at[bc_cols : bc_cols + heads], gdt_ref),
+        (gnorm_in, gnorm_ref), (gtaps_in, gtaps_ref), (gbias_in, gbias_ref),
+        (ggate_in, ggate_ref), (gbct_in, gbct_ref), (gbcb_in, gbcb_ref), (gdtb_in, gdtb_ref),
+        (galog_in, galog_ref), (gskip_in, gskip_ref), (zx, gzx_ref),
+    )
+    copies = [
+        pltpu.make_async_copy(source, target, sems.at[k])
+        for k, (source, target) in enumerate(moves)
+    ]
+    for copy in copies[:-1]:
+        copy.start()
+    for part in range(2):
+        zx[:, part, :] = gzx_in[:, part * inner : (part + 1) * inner]
+    copies[-1].start()
+    for copy in copies:
+        copy.wait()
+
+
+def fused(
+    x_in, cotangent, seq_ids, norm_gain, w_zx, w_bc, w_dt, w_out_t, conv_x_weight, conv_x_bias,
+    conv_bc_weight, conv_bc_bias, dt_bias, a_log, d_skip, gate_gain,
+):
+    rows, share = x_in.shape
+    held, _, inner = w_zx.shape
+    bc_cols, heads, taps = w_bc.shape[1], w_dt.shape[1], conv_x_weight.shape[0]
+    dp, tensor = lax.axis_size("dp"), lax.axis_size("tensor")
+    highs = {name: lines(name)[3] for name in ("dp", "tensor")}
+    width = share * tensor
+    state = bc_cols * tensor // 2
+    tile, chunks, pairs = 128, rows // 128, inner // 128
+    side_rows = 16 * -(-(bc_cols + heads + 1) // 16)
+    hbm = pl.BlockSpec(memory_space=pltpu.HBM)
+    vmem = pl.BlockSpec(memory_space=pltpu.VMEM)
+
+    def v(*dims, dtype=F32):
+        return pltpu.VMEM(dims, dtype)
+
+    def h(*dims):
+        return pltpu.VMEM(dims, BF16)
+
+    def sem(*dims):
+        return pltpu.SemaphoreType.DMA(dims)
+
+    high = highs["dp"]
+    scratch = dict(
+        xr=h(rows, width), cr=h(rows, width),
+        side=h(dp, side_rows, held), wx=h(dp, held, inner), wz=h(dp, held, inner),
+        wo=h(dp, held, inner),
+        xs_sems=sem(4, 2, highs["tensor"]), cs_sems=sem(4, 2, highs["tensor"]),
+        side_sems=sem(4, 2, high), wx_sems=sem(4, 2, high), wz_sems=sem(4, 2, high),
+        wo_sems=sem(4, 2, high), own_sems=sem(6),
+        seg=v(rows, tile), mask=v(taps - 1, rows, tile), link=h(rows, rows),
+        inv=v(rows, tile), normed=h(rows, width), nt=h(width, rows), ct=h(width, rows),
+        bcpre=v(bc_cols, rows), bcown=h(bc_cols, rows), bct=h(tensor, bc_cols, rows),
+        bc_sems=sem(2, tensor), dtin=v(heads, rows), ld=v(heads, rows),
+        cum=v(heads, rows), cumc=v(rows, tile),
+        stepw=v(rows, inner), entw=v(rows, inner), tailw=v(rows, inner),
+        xpre=v(rows, inner), val=v(rows, inner), act=v(rows, inner),
+        vb=h(rows, inner), xt=h(rows, inner), bm=h(rows, state), cm=h(rows, state),
+        state=v(state, inner), prior=h(chunks, state, inner),
+        decay=v(chunks, pairs, tile, 2 * tile), wst=h(chunks, pairs, 2 * tile, tile),
+        ynos=v(rows, inner), z=v(rows, inner), gated=v(rows, inner), q=h(rows, inner),
+        wide=v(rows, tile), stat=v(3, 8, rows), stat_slots=v(3, tensor - 1, 8, rows),
+        stat_sems=sem(2, 3 * tensor), rs=v(rows, tile), pull=v(rows, tile),
+        dq=v(rows, inner), dz=h(rows, inner), dy=v(rows, inner), edy=h(rows, inner),
+        dv=v(rows, inner), dvc=v(rows, inner), through=v(chunks, 8, inner),
+        dx=h(rows, inner), dbc=v(2 * state, rows),
+        dbc_send=h(tensor, bc_cols, rows), dbc_slots=h(tensor - 1, bc_cols, rows),
+        dbc_sems=sem(2, tensor), dside=h(side_rows, rows), meanw=v(rows, tile),
+        gpart=v(dp, 8, held), sums=v(16, inner), sums_two=v(16, inner), sum_pair=v(16, inner),
+        sum_slots=v(high - 1, 16, inner),
+        sum_sems=sem(2, dp), gsum=v(dp, held), gain_slots=v(tensor - 1, dp, held),
+        gain_sems=sem(2, tensor),
+        op_send=h(tensor, rows, share), op_slots=h(tensor - 1, rows, share),
+        op_own=v(rows, share), op_sems=sem(2, tensor),
+        np_send=h(tensor, rows, share), np_slots=h(tensor - 1, rows, share),
+        np_own=v(rows, share), np_sems=sem(2, tensor),
+        go_send=h(dp, held, inner), go_pair=h(high, held, inner), go_held=h(high, held, inner),
+        go_land=h(high, held, inner), go_sems=sem(4, high),
+        gz_send=h(dp, held, inner), gz_pair=h(high, held, inner), gz_held=h(high, held, inner),
+        gz_land=h(high, held, inner), gz_sems=sem(4, high),
+        gx_send=h(dp, held, inner), gx_pair=h(high, held, inner), gx_held=h(high, held, inner),
+        gx_land=h(high, held, inner), gx_sems=sem(4, high),
+        gs_send=h(dp, side_rows, held), gs_pair=h(high, side_rows, held), gs_held=h(high, side_rows, held),
+        gs_land=h(high, side_rows, held), gs_sems=sem(4, high),
+        sideown=h(side_rows, held), cols=v(tile, tile),
+        wbc_in=h(bc_cols, held), wdt_in=h(heads, held), norm_in=h(1, held),
+        seq_in=v(1, rows, dtype=jnp.int32), taps_in=v(taps, inner), bias_in=v(1, inner),
+        bct_in=v(taps, bc_cols), bcb_in=v(1, bc_cols), dtb_in=v(1, heads), alog_in=v(1, heads),
+        skip_in=v(1, heads), gain_in=v(1, inner), fetch_sems=sem(12),
+    )
+    results = pl.pallas_call(
+        layer_kernel,
+        in_specs=[vmem] + [hbm] * 15,
+        out_specs=[vmem] * 14,
+        out_shape=[
+            shape((rows, share), BF16), shape((rows, share)), shape((held, 2 * inner)),
+            shape((side_rows, held)), shape((held, inner)), shape((1, held)),
+            shape((taps, inner)), shape((1, inner)), shape((1, inner)), shape((taps, bc_cols)),
+            shape((1, bc_cols)), shape((1, heads)), shape((1, heads)), shape((1, heads)),
+        ],
+        scratch_shapes=[scratch],
+        compiler_params=pltpu.CompilerParams(
+            collective_id=0, has_side_effects=True, vmem_limit_bytes=50 * 1024 * 1024
+        ),
+        name="whole_layer",
+    )(
+        w_zx.reshape(held, 2 * inner),
+        *(
+            pltpu.with_memory_space_constraint(array, pltpu.HBM)
+            for array in (
+                x_in, cotangent, w_out_t, w_bc.T, w_dt.T, norm_gain[None, :], seq_ids[None, :],
+                conv_x_weight, conv_x_bias[None, :], conv_bc_weight, conv_bc_bias[None, :],
+                dt_bias[None, :], a_log[None, :], d_skip[None, :], gate_gain[None, :],
+            )
+        ),
+    )
+    finished = [
+        shape((rows, share), BF16), shape((rows, share)), shape((held, 2, inner)),
+        shape((bc_cols, held)), shape((heads, held)), shape((held, inner)), shape((1, held)),
+        shape((taps, inner)), shape((1, inner)), shape((1, inner)), shape((taps, bc_cols)),
+        shape((1, bc_cols)), shape((1, heads)), shape((1, heads)), shape((1, heads)),
+    ]
+    results = pl.pallas_call(
+        finish_kernel,
+        in_specs=[vmem] * 14,
+        out_specs=[hbm] * len(finished),
+        out_shape=finished,
+        scratch_shapes=[v(held, 2, inner), sem(len(finished))],
+        compiler_params=pltpu.CompilerParams(vmem_limit_bytes=12 * 1024 * 1024),
+        name="layer_finish",
+    )(*results)
+    out, grad, gzx, gbc, gdt, gwo, gnorm, gtaps, gbias, ggate, gbct, gbcb, gdtb, galog, gskip = (
+        results
+    )
+    return (
+        out, grad, gnorm[0], gzx, gbc.T, gdt.T, gwo, gtaps, gbias[0], gbct, gbcb[0], gdtb[0],
+        galog[0], gskip[0], ggate[0],
+    )
+
+
+def fits(x_in, w_zx, w_bc, w_dt, w_out_t, taps, tensor_count):
+    rows, share = x_in.shape
+    held, inner = w_out_t.shape
+    bc_cols, heads = w_bc.shape[1], w_dt.shape[1]
+    dp_count = lax.axis_size("dp")
+    return (
+        held == 128 and share % held == 0 and rows % 128 == 0 and inner % 128 == 0
+        and dp_count == 8 and heads == 8 and bc_cols % 16 == 0 and taps == 4
+        and tensor_count % 2 == 0 and bc_cols * tensor_count == 256
+        and inner == heads * HEAD_DIM
+    )
+
+
 def local(
     x_in,
     cotangent,
@@ -520,6 +1551,11 @@
     *,
     tensor_count,
 ):
+    if fits(x_in, w_zx, w_bc, w_dt, w_out_t, conv_x_weight.shape[0], tensor_count):
+        return fused(
+            x_in, cotangent, seq_ids, norm_gain, w_zx, w_bc, w_dt, w_out_t, conv_x_weight, conv_x_bias,
+            conv_bc_weight, conv_bc_bias, dt_bias, a_log, d_skip, gate_gain,
+        )
     rows, share = x_in.shape
     width = share * tensor_count
     inner = w_out_t.shape[1]

time: 217 us -> 97.2 us (0.45)
  Pallas kernels: 147 us -> 94.7 us
  local copies, waits for them, and re-layouts: 31.6 us -> 0.98 us
  matrix products: 20.6 us -> 0 us
  other arithmetic: 10.7 us -> 0 us
  blocking collectives: 5.96 us -> 0 us
    pallas_call x7 -> x2, Pallas kernels: 147 us -> 94.7 us  [the longest x1 93.4 us: fused(): pl.pallas_call(layer_kernel, in_specs=[vmem] + [hbm] * 15, out_specs=[vme...]
    dot_general x9 -> x0, matrix products: 20.6 us -> none  [the longest x3 8.64 us: plain_product(): lax.dot_general(left, right, (((1,), (0,)), ((), ())), preferred_element_...]
    reshape x14 -> x0, local copies, waits for them, and re-layouts: 6.86 us -> none  [the longest x2 1.5 us: local(): cum_pairs = cumulative.reshape(rows, pairs, 2).transpose(1, 0, 2)]
    all_gather x1 -> x0, blocking collectives: 5.96 us -> none  [local(): bc_act = lax.all_gather(bc_local, 'tensor', axis=1, tiled=True)]
    unnamed x56 -> x1, local copies, waits for them, and re-layouts: 6.44 us -> 0.98 us
    concatenate x6 -> x0, local copies, waits for them, and re-layouts: 5.41 us -> none  [the longest x1 2.58 us: local(): jnp.concatenate([d_z, d_x, d_bcpre, d_dt.astype(BF16), jnp.zeros((rows, s...]
    concatenate x5 -> x0, other arithmetic: 4.72 us -> none  [the longest x1 2.03 us: local(): jnp.concatenate([pack_grad, out_grad], axis=1)]
    slice x10 -> x0, local copies, waits for them, and re-layouts: 4.11 us -> none  [the longest x6 2.34 us: local(): parts.append(flat[at_piece:at_piece + piece.shape[0]])]
where the time goes in v1:
time: 97.2 us; the launch traced here: 96.5 us
  Pallas kernels  94.7 us (97%)
  local copies, waits for them, and re-layouts  0.98 us (1%)
    pallas_call x1, Pallas kernels, fused(): pl.pallas_call(layer_kernel, in_specs=[vmem] + [hbm] * 15, out_specs=[vme...  93.4 us

profile of v1, /device:TPU:0, one launch (start us, length us, event | category | flops | bytes accessed | tf_op | source)
XLA Modules:
  0.0 96.5 jit_solution(4480537174498305141)
XLA Ops:
  0.6 1.0 %copy.31 = bf16[16,8,2,512]{3,1,2,0:T(8,128)(2,1)S(1)} copy(bf16[16,8,2,512]{3,2,1,0:T(2,128)(2,1)} %bitcast.22) | data formatting | bytes 524288
  1.6 93.4 %whole_layer.1 = (bf16[512,256]{1,0:T(8,128)(2,1)S(1)}, f32[512,256]{1,0:T(8,128)S(1)}, f32[128,1024]{1,0:T(8,128)S(1)}, f32[80,128]{1,0:T(8,128)S(1)}, f32[128,...) custom-call(bf16[128,1024]{1,0:T(8,128)(2,1)S(1)} %bitcast.21, ...), custom_call_target="tpu_custom_call" | custom-call | tf_op jit(solution)/shard_map/whole_layer/pallas_call | solution.py:1471
  95.0 1.3 %layer_finish.1 = (bf16[512,256]{1,0:T(8,128)(2,1)}, f32[512,256]{1,0:T(8,128)}, f32[128,2,512]{2,1,0:T(2,128)}, f32[64,128]{1,0:T(8,128)}, f32[8,128]{1,0:T(8,1...) custom-call(bf16[512,256]{1,0:T(8,128)(2,1)S(1)} %get-tuple-element., ...), custom_call_target="tpu_custom_call" | custom-call | tf_op jit(solution)/shard_map/layer_finish/pallas_call | solution.py:1503
